TPU v7x, 32 devices: a whole 2x2x4 slice. The times are simulated.
32 devices in a mesh: rep: 4 (over y, x), grp: 8 (over z, core).
Axes of the slice: x: 2, y: 2, z: 4, core: 2. Of those that a mesh axis runs over, the one named last changes fastest.
Arguments:
- block_in: bfloat16 [2, 4, 1024, 1024], P(None, 'rep', 'grp'), may hold values from -6 to 6
- cotangent: bfloat16 [2, 4, 1024, 1024], P(None, 'rep', 'grp'), may hold values from -6 to 6
- w_qkv: bfloat16 [2, 1024, 3072], P(None, 'grp'), may hold values from -0.1875 to 0.1875
- w_out: bfloat16 [2, 1024, 1024], P(None, 'grp'), may hold values from -0.1875 to 0.1875
- w_up: bfloat16 [2, 1024, 4096], P(None, 'grp'), may hold values from -0.1875 to 0.1875
- w_down: bfloat16 [2, 4096, 1024], P(None, 'grp'), may hold values from -0.09375 to 0.09375
- norm_gains: bfloat16 [2, 1024, 4], P(None, 'grp'), may hold values from 0.25 to 1.75
Outputs:
- block_out: bfloat16 [2, 4, 1024, 1024], P(None, 'rep', 'grp')
- block_in_grad: float32 [2, 4, 1024, 1024], P(None, 'rep', 'grp')
- w_qkv_grad: float32 [2, 1024, 3072], P(None, 'grp')
- w_out_grad: float32 [2, 1024, 1024], P(None, 'grp')
- w_up_grad: float32 [2, 1024, 4096], P(None, 'grp')
- w_down_grad: float32 [2, 4096, 1024], P(None, 'grp')
- norm_gains_grad: float32 [2, 1024, 4], P(None, 'grp')
All inputs are finite; a program needn't handle non-finite values.
Results may differ from a plain program's by a relative error of at most 0.023.
Values may be sent and summed in bfloat16 or wider, within the bound.
A program may use at most 384 MiB of HBM per device.

v0:
```python
import jax
import jax.numpy as jnp
from jax import lax
from jax.sharding import PartitionSpec as P

HEADS = 16
HDIM = 64


EPS = 1e-06
NEGATIVE = -1e30


def norm_apply(values, gains):
    return values * lax.rsqrt(jnp.mean(values * values, axis=-1, keepdims=True) + EPS) * gains


def inner_rows(left, right):
    return lax.dot_general(
        left, right, (((0,), (0,)), ((), ())), preferred_element_type=jnp.float32
    )


def times_trans(left, right):
    return lax.dot_general(
        left, right, (((1,), (1,)), ((), ())), preferred_element_type=jnp.float32
    )


def split_blocks(whole):
    length = whole.shape[0]
    width = min(512, length)
    count = length // width
    return (whole.reshape(count, width, HEADS, HDIM), width, count)


def block_at(blocks, index):
    return lax.dynamic_index_in_dim(blocks, index, 0, keepdims=False)


def key_scores(query, key_block, key_start, query_pos):
    scale = HDIM ** (-0.5)
    scores = (
        jnp.einsum("qhd,khd->hqk", query, key_block, preferred_element_type=jnp.float32) * scale
    )
    key_pos = key_start + jnp.arange(key_block.shape[0], dtype=jnp.int32)
    allowed = key_pos[None, :] <= query_pos[:, None]
    return (scores, allowed[None])


def attend(query, keys_all, values_all, query_pos):
    key_blocks, width, count = split_blocks(keys_all)
    value_blocks = split_blocks(values_all)[0]
    row_count = query.shape[0]
    upper = query_pos[row_count - 1] // width + 1

    def total_step(index, carry):
        running, total = carry
        scores, allowed = key_scores(query, block_at(key_blocks, index), index * width, query_pos)
        newest = jnp.maximum(running, jnp.max(jnp.where(allowed, scores, NEGATIVE), axis=-1))
        terms = jnp.where(allowed, jnp.exp(scores - newest[..., None]), 0.0)
        total = total * jnp.exp(running - newest) + jnp.sum(terms, axis=-1)
        return (newest, total)

    start_run = jnp.full((HEADS, row_count), NEGATIVE, jnp.float32)
    start_total = jnp.zeros((HEADS, row_count), jnp.float32)
    running, total = lax.fori_loop(0, upper, total_step, (start_run, start_total))
    log_total = running + jnp.log(total)

    def mix_step(index, accum):
        scores, allowed = key_scores(query, block_at(key_blocks, index), index * width, query_pos)
        probs = jnp.where(allowed, jnp.exp(scores - log_total[..., None]), 0.0)
        return accum + jnp.einsum(
            "hqk,khd->qhd",
            probs.astype(jnp.bfloat16),
            block_at(value_blocks, index),
            preferred_element_type=jnp.float32,
        )

    start_mix = jnp.zeros((row_count, HEADS, HDIM), jnp.float32)
    mixed = lax.fori_loop(0, upper, mix_step, start_mix)
    return (mixed.reshape(row_count, HEADS * HDIM), log_total)


def attend_back(query, keys_all, values_all, log_total, out_grad, delta, query_pos):
    key_blocks, width, count = split_blocks(keys_all)
    value_blocks = split_blocks(values_all)[0]
    row_count = query.shape[0]
    upper = query_pos[row_count - 1] // width + 1
    scale = HDIM ** (-0.5)

    def back_step(index, carry):
        query_acc, pieces = carry
        key_block = block_at(key_blocks, index)
        value_block = block_at(value_blocks, index)
        scores, allowed = key_scores(query, key_block, index * width, query_pos)
        probs = jnp.where(allowed, jnp.exp(scores - log_total[..., None]), 0.0)
        prob_grad = jnp.einsum(
            "qhd,khd->hqk", out_grad, value_block, preferred_element_type=jnp.float32
        )
        score_grad = (probs * (prob_grad - delta[..., None])).astype(jnp.bfloat16)
        query_acc = (
            query_acc
            + jnp.einsum("hqk,khd->qhd", score_grad, key_block, preferred_element_type=jnp.float32)
            * scale
        )
        key_grad = (
            jnp.einsum("hqk,qhd->khd", score_grad, query, preferred_element_type=jnp.float32)
            * scale
        )
        value_grad = jnp.einsum(
            "hqk,qhd->khd", probs.astype(jnp.bfloat16), out_grad, preferred_element_type=jnp.float32
        )
        joined = jnp.concatenate(
            [key_grad.reshape(width, HEADS * HDIM), value_grad.reshape(width, HEADS * HDIM)], axis=1
        )
        pieces = lax.dynamic_update_index_in_dim(pieces, joined, index, 0)
        return (query_acc, pieces)

    start_acc = jnp.zeros((row_count, HEADS, HDIM), jnp.float32)
    start_pieces = jnp.zeros((count, width, 2 * HEADS * HDIM), jnp.float32)
    query_grad, pieces = lax.fori_loop(0, upper, back_step, (start_acc, start_pieces))
    return (query_grad.reshape(row_count, HEADS * HDIM), pieces.reshape(-1, pieces.shape[-1]))


def layer_forward(hidden_in, weights, query_pos):
    w_qkv_full, w_out_full, w_up_full, w_down_full, gain_full = weights
    gains_f = gain_full.astype(jnp.float32)
    row_count = hidden_in.shape[0]
    width = w_out_full.shape[1]
    normed = norm_apply(hidden_in, gains_f[:, 0]).astype(jnp.bfloat16)
    qkv_low = jnp.dot(normed, w_qkv_full, preferred_element_type=jnp.float32).astype(jnp.bfloat16)
    query = qkv_low[:, :width]
    keys_all, values_all = (
        lax.all_gather(qkv_low[:, width : 2 * width], "grp", axis=0, tiled=True),
        lax.all_gather(qkv_low[:, 2 * width :], "grp", axis=0, tiled=True),
    )
    mixed, log_total = attend(
        query.reshape(row_count, HEADS, HDIM),
        keys_all.reshape(-1, HEADS, HDIM),
        values_all.reshape(-1, HEADS, HDIM),
        query_pos,
    )
    mixed_low = mixed.astype(jnp.bfloat16)
    attn_out = jnp.dot(mixed_low, w_out_full, preferred_element_type=jnp.float32)
    resid = hidden_in + norm_apply(attn_out, gains_f[:, 1])
    mlp_in = norm_apply(resid, gains_f[:, 2]).astype(jnp.bfloat16)
    up_out = jnp.dot(mlp_in, w_up_full, preferred_element_type=jnp.float32)
    active = jax.nn.gelu(up_out).astype(jnp.bfloat16)
    down_out = jnp.dot(active, w_down_full, preferred_element_type=jnp.float32)
    result = resid + norm_apply(down_out, gains_f[:, 3])
    kept = (
        hidden_in,
        normed,
        qkv_low,
        mixed,
        mixed_low,
        log_total,
        attn_out,
        resid,
        mlp_in,
        up_out,
        active,
        down_out,
    )
    return (result, kept)


def layer_backward(grad_out, weights, kept, query_pos):
    w_qkv_full, w_out_full, w_up_full, w_down_full, gain_full = weights
    (
        hidden_in,
        normed,
        qkv_low,
        mixed,
        mixed_low,
        log_total,
        attn_out,
        resid,
        mlp_in,
        up_out,
        active,
        down_out,
    ) = kept
    gains_f = gain_full.astype(jnp.float32)
    row_count = hidden_in.shape[0]
    width = w_out_full.shape[1]
    unused, puller = jax.vjp(norm_apply, down_out, gains_f[:, 3])
    down_grad, gain_four = puller(grad_out)
    down_low = down_grad.astype(jnp.bfloat16)
    w_down_grad = inner_rows(active, down_low)
    active_grad = times_trans(down_low, w_down_full)
    unused, puller = jax.vjp(jax.nn.gelu, up_out)
    up_low = puller(active_grad)[0].astype(jnp.bfloat16)
    w_up_grad = inner_rows(mlp_in, up_low)
    mlp_grad = times_trans(up_low, w_up_full)
    unused, puller = jax.vjp(norm_apply, resid, gains_f[:, 2])
    resid_part, gain_three = puller(mlp_grad)
    resid_grad = grad_out + resid_part
    unused, puller = jax.vjp(norm_apply, attn_out, gains_f[:, 1])
    attn_grad, gain_two = puller(resid_grad)
    attn_low = attn_grad.astype(jnp.bfloat16)
    w_out_grad = inner_rows(mixed_low, attn_low)
    mixed_grad = times_trans(attn_low, w_out_full).astype(jnp.bfloat16)
    keys_all, values_all = (
        lax.all_gather(qkv_low[:, width : 2 * width], "grp", axis=0, tiled=True),
        lax.all_gather(qkv_low[:, 2 * width :], "grp", axis=0, tiled=True),
    )
    delta = jnp.sum(
        (mixed_grad.astype(jnp.float32) * mixed).reshape(row_count, HEADS, HDIM), axis=-1
    ).T
    query_low = qkv_low[:, :width]
    query_grad, key_value_terms = attend_back(
        query_low.reshape(row_count, HEADS, HDIM),
        keys_all.reshape(-1, HEADS, HDIM),
        values_all.reshape(-1, HEADS, HDIM),
        log_total,
        mixed_grad.reshape(row_count, HEADS, HDIM),
        delta,
        query_pos,
    )
    key_value_grad = lax.psum_scatter(
        key_value_terms.astype(jnp.bfloat16), "grp", scatter_dimension=0, tiled=True
    ).astype(jnp.float32)
    qkv_grad = jnp.concatenate([query_grad, key_value_grad], axis=1).astype(jnp.bfloat16)
    w_qkv_grad = inner_rows(normed, qkv_grad)
    normed_grad = times_trans(qkv_grad, w_qkv_full)
    unused, puller = jax.vjp(norm_apply, hidden_in, gains_f[:, 0])
    input_part, gain_one = puller(normed_grad)
    gain_grad = jnp.stack([gain_one, gain_two, gain_three, gain_four], axis=1)
    return (resid_grad + input_part, (w_qkv_grad, w_out_grad, w_up_grad, w_down_grad, gain_grad))


def body(block_in, cotangent, w_qkv, w_out, w_up, w_down, norm_gains):
    layer_count = w_qkv.shape[0]
    micro_count = block_in.shape[0]
    row_count = block_in.shape[2]
    query_pos = lax.axis_index("grp") * row_count + jnp.arange(row_count, dtype=jnp.int32)
    totals = [None] * layer_count
    outputs = []
    input_grads = []
    for micro_idx in range(micro_count):
        hidden = block_in[micro_idx, 0].astype(jnp.float32)
        saved = []
        for layer_idx in range(layer_count):
            hidden, kept = layer_forward(
                hidden,
                (
                    lax.all_gather(w_qkv[layer_idx], "grp", axis=0, tiled=True),
                    lax.all_gather(w_out[layer_idx], "grp", axis=0, tiled=True),
                    lax.all_gather(w_up[layer_idx], "grp", axis=0, tiled=True),
                    lax.all_gather(w_down[layer_idx], "grp", axis=0, tiled=True),
                    lax.all_gather(norm_gains[layer_idx], "grp", axis=0, tiled=True),
                ),
                query_pos,
            )
            saved.append(kept)
        outputs.append(hidden.astype(jnp.bfloat16))
        grad_flow = cotangent[micro_idx, 0].astype(jnp.float32)
        for layer_idx in reversed(range(layer_count)):
            grad_flow, parts = layer_backward(
                grad_flow,
                (
                    lax.all_gather(w_qkv[layer_idx], "grp", axis=0, tiled=True),
                    lax.all_gather(w_out[layer_idx], "grp", axis=0, tiled=True),
                    lax.all_gather(w_up[layer_idx], "grp", axis=0, tiled=True),
                    lax.all_gather(w_down[layer_idx], "grp", axis=0, tiled=True),
                    lax.all_gather(norm_gains[layer_idx], "grp", axis=0, tiled=True),
                ),
                saved[layer_idx],
                query_pos,
            )
            if totals[layer_idx] is None:
                totals[layer_idx] = parts
            else:
                totals[layer_idx] = tuple(
                    (left + right for left, right in zip(totals[layer_idx], parts))
                )
        input_grads.append(grad_flow)
    reduced = []
    for layer_idx in range(layer_count):
        accum = totals[layer_idx]
        shards = (
            lax.psum_scatter(
                accum[0].astype(jnp.bfloat16), "grp", scatter_dimension=0, tiled=True
            ).astype(jnp.float32),
            lax.psum_scatter(
                accum[1].astype(jnp.bfloat16), "grp", scatter_dimension=0, tiled=True
            ).astype(jnp.float32),
            lax.psum_scatter(
                accum[2].astype(jnp.bfloat16), "grp", scatter_dimension=0, tiled=True
            ).astype(jnp.float32),
            lax.psum_scatter(
                accum[3].astype(jnp.bfloat16), "grp", scatter_dimension=0, tiled=True
            ).astype(jnp.float32),
            lax.psum_scatter(
                accum[4].astype(jnp.bfloat16), "grp", scatter_dimension=0, tiled=True
            ).astype(jnp.float32),
        )
        reduced.append(
            (
                lax.psum(shards[0].astype(jnp.bfloat16), "rep").astype(jnp.float32),
                lax.psum(shards[1].astype(jnp.bfloat16), "rep").astype(jnp.float32),
                lax.psum(shards[2].astype(jnp.bfloat16), "rep").astype(jnp.float32),
                lax.psum(shards[3].astype(jnp.bfloat16), "rep").astype(jnp.float32),
                lax.psum(shards[4].astype(jnp.bfloat16), "rep").astype(jnp.float32),
            )
        )
    block_out = jnp.stack(outputs)[:, None]
    block_in_grad = jnp.stack(input_grads)[:, None]
    stacked = [
        jnp.stack([reduced[layer_idx][member] for layer_idx in range(layer_count)])
        for member in range(5)
    ]
    return (block_out, block_in_grad, stacked[0], stacked[1], stacked[2], stacked[3], stacked[4])


def solution(mesh):
    return jax.shard_map(
        body,
        mesh=mesh,
        in_specs=(
            P(None, "rep", "grp", None),
            P(None, "rep", "grp", None),
            P(None, "grp", None),
            P(None, "grp", None),
            P(None, "grp", None),
            P(None, "grp", None),
            P(None, "grp", None),
        ),
        out_specs=(
            P(None, "rep", "grp", None),
            P(None, "rep", "grp", None),
            P(None, "grp", None),
            P(None, "grp", None),
            P(None, "grp", None),
            P(None, "grp", None),
            P(None, "grp", None),
        ),
        check_vma=False,
    )
```

profile of v0, /device:TPU:0, one launch (start us, length us, event | category | flops | bytes accessed | tf_op | source)
XLA Modules:
  0.0 1937.6 jit_solution(5514778637835726931)
XLA Ops:
  10.0 13.4 all-gather
  23.7 54.0 %all-gather.43.cloned.1.call-done = bf16[1,1024,3072]{2,1,0:T(8,128)(2,1)} async-done(((bf16[1,128,3072]{2,1,0:T(8,128)(2,1)}), bf16[1,1024,3072]{2,1,0:T(8,128)(2,1)}) %all-gather.43.cloned.1.call-update) | async-done | bytes 6291472 | tf_op jit(solution)/shard_map/all_gather | solution.py:249
  98.6 9.1 all-gather.5
  110.4 6.3 reshape.879
  123.4 17.8 all-gather.35.cloned.1.call-done
  141.3 6.3 reshape.878
  147.6 5.6 copy.236
  156.6 15.3 all-gather.45.cloned.1.call-done
  174.8 27.8 %all-gather.29.cloned.1.call-done = bf16[1024,1024]{1,0:T(8,128)(2,1)} async-done(((bf16[128,1024]{1,0:T(8,128)(2,1)}), bf16[1024,1024]{1,0:T(8,128)(2,1)}) %all-gather.29.cloned.1.call-update) | async-done | bytes 2097168 | tf_op jit(solution)/shard_map/all_gather | solution.py:135
  202.6 6.3 reshape.875
  214.5 18.2 all-gather.27.cloned.1.call-done
  232.7 6.3 reshape.874
  239.0 5.8 copy.224
  255.1 60.7 %all-gather.47.cloned.1.call-done = bf16[1,1024,4096]{2,1,0:T(8,128)(2,1)} async-done(((bf16[1,128,4096]{2,1,0:T(8,128)(2,1)}), bf16[1,1024,4096]{2,1,0:T(8,128)(2,1)}) %all-gather.47.cloned.1.call-update) | async-done | bytes 8388624 | tf_op jit(solution)/shard_map/all_gather | solution.py:251
  320.6 78.0 %all-gather.49.cloned.1.call-done = bf16[1,4096,1024]{2,1,0:T(8,128)(2,1)} async-done(((bf16[1,512,1024]{2,1,0:T(8,128)(2,1)}), bf16[1,4096,1024]{2,1,0:T(8,128)(2,1)}) %all-gather.49.cloned.1.call-update) | async-done | bytes 8388624 | tf_op jit(solution)/shard_map/all_gather | solution.py:252
  404.2 5.6 fusion.230
  413.7 49.9 %all-gather.51.cloned.1.call-done = bf16[1,1024,3072]{2,1,0:T(8,128)(2,1)} async-done(((bf16[1,128,3072]{2,1,0:T(8,128)(2,1)}), bf16[1,1024,3072]{2,1,0:T(8,128)(2,1)}) %all-gather.51.cloned.1.call-update) | async-done | bytes 6291472 | tf_op jit(solution)/shard_map/all_gather | solution.py:249
  477.1 19.1 all-gather.33.cloned.1.call-done
  496.2 6.3 reshape.877
  509.4 17.1 all-gather.41.cloned.1.call-done
  526.5 6.3 reshape.881
  532.9 5.5 copy.243
  538.4 18.2 all-gather.39.cloned.1.call-done
  556.6 6.3 reshape.880
  563.0 5.6 copy.242
  568.6 18.9 all-gather.31.cloned.1.call-done
  587.5 6.3 reshape.876
  611.7 5.8 all-gather.53.cloned.1.call-done
  622.5 78.0 %all-gather.55.cloned.1.call-done = bf16[1,1024,4096]{2,1,0:T(8,128)(2,1)} async-done(((bf16[1,128,4096]{2,1,0:T(8,128)(2,1)}), bf16[1,1024,4096]{2,1,0:T(8,128)(2,1)}) %all-gather.55.cloned.1.call-update) | async-done | bytes 8388624 | tf_op jit(solution)/shard_map/all_gather | solution.py:251
  700.5 6.0 fusion.212
  706.6 76.6 %all-gather.57.cloned.1.call-done = bf16[1,4096,1024]{2,1,0:T(8,128)(2,1)} async-done(((bf16[1,512,1024]{2,1,0:T(8,128)(2,1)}), bf16[1,4096,1024]{2,1,0:T(8,128)(2,1)}) %all-gather.57.cloned.1.call-update) | async-done | bytes 8388624 | tf_op jit(solution)/shard_map/all_gather | solution.py:252
  783.2 5.7 multiply_reduce_fusion.24
  799.4 7.1 fusion.273
  806.5 7.5 fusion.287
  836.6 17.2 while.158
  857.3 18.7 while.156
  879.6 39.9 %reduce-scatter.23.cloned.1.call-done = bf16[128,2048]{1,0:T(8,128)(2,1)} async-done(((bf16[1024,2048]{1,0:T(8,128)(2,1)}), bf16[128,2048]{1,0:T(8,128)(2,1)}) %reduce-scatter.23.cloned.1.call-update) | async-done | bytes 524304 | tf_op jit(solution)/shard_map/reduce_scatter | solution.py:222
  919.5 6.0 fusion.232
  925.6 44.9 %reduce-scatter.19.cloned.1.call-done = bf16[128,2048]{1,0:T(8,128)(2,1)} async-done(((bf16[1024,2048]{1,0:T(8,128)(2,1)}), bf16[128,2048]{1,0:T(8,128)(2,1)}) %reduce-scatter.19.cloned.1.call-update) | async-done | bytes 524304 | tf_op jit(solution)/shard_map/reduce_scatter | solution.py:222
  970.5 6.1 multiply_reduce_fusion.5
  979.7 7.1 fusion.266
  1005.5 17.1 while.157
  1031.6 17.4 while.159
  1058.4 9.3 fusion.407
  1067.7 9.7 add_convert_fusion
  1078.5 9.5 fusion.405
  1088.0 11.5 add_convert_fusion.2
  1109.8 9.3 fusion.406
  1119.1 9.6 add_convert_fusion.1
  1129.7 9.5 fusion.404
  1139.3 11.5 add_convert_fusion.3
  1151.9 7.5 fusion.360
  1159.4 9.4 add_convert_fusion.5
  1181.9 30.3 %reduce-scatter.31.cloned.1.call-done = bf16[128,1024]{1,0:T(8,128)(2,1)} async-done(((bf16[1024,1024]{1,0:T(8,128)(2,1)}), bf16[128,1024]{1,0:T(8,128)(2,1)}) %reduce-scatter.31.cloned.1.call-update) | async-done | bytes 262160 | tf_op jit(solution)/shard_map/reduce_scatter | solution.py:287
  1212.2 90.7 %reduce-scatter.41.cloned.1.call-done = bf16[512,1024]{1,0:T(8,128)(2,1)} async-done(((bf16[4096,1024]{1,0:T(8,128)(2,1)}), bf16[512,1024]{1,0:T(8,128)(2,1)}) %reduce-scatter.41.cloned.1.call-update) | async-done | bytes 1048592 | tf_op jit(solution)/shard_map/reduce_scatter | solution.py:293
  1302.9 90.1 %reduce-scatter.37.cloned.1.call-done = bf16[128,4096]{1,0:T(8,128)(2,1)} async-done(((bf16[1024,4096]{1,0:T(8,128)(2,1)}), bf16[128,4096]{1,0:T(8,128)(2,1)}) %reduce-scatter.37.cloned.1.call-update) | async-done | bytes 1048592 | tf_op jit(solution)/shard_map/reduce_scatter | solution.py:290
  1393.0 70.5 %reduce-scatter.29.cloned.1.call-done = bf16[128,3072]{1,0:T(8,128)(2,1)} async-done(((bf16[1024,3072]{1,0:T(8,128)(2,1)}), bf16[128,3072]{1,0:T(8,128)(2,1)}) %reduce-scatter.29.cloned.1.call-update) | async-done | bytes 786448 | tf_op jit(solution)/shard_map/reduce_scatter | solution.py:284
  1463.5 90.2 %reduce-scatter.39.cloned.1.call-done = bf16[512,1024]{1,0:T(8,128)(2,1)} async-done(((bf16[4096,1024]{1,0:T(8,128)(2,1)}), bf16[512,1024]{1,0:T(8,128)(2,1)}) %reduce-scatter.39.cloned.1.call-update) | async-done | bytes 1048592 | tf_op jit(solution)/shard_map/reduce_scatter | solution.py:293
  1553.7 90.1 %reduce-scatter.35.cloned.1.call-done = bf16[128,4096]{1,0:T(8,128)(2,1)} async-done(((bf16[1024,4096]{1,0:T(8,128)(2,1)}), bf16[128,4096]{1,0:T(8,128)(2,1)}) %reduce-scatter.35.cloned.1.call-update) | async-done | bytes 1048592 | tf_op jit(solution)/shard_map/reduce_scatter | solution.py:290
  1643.8 70.5 %reduce-scatter.27.cloned.1.call-done = bf16[128,3072]{1,0:T(8,128)(2,1)} async-done(((bf16[1024,3072]{1,0:T(8,128)(2,1)}), bf16[128,3072]{1,0:T(8,128)(2,1)}) %reduce-scatter.27.cloned.1.call-update) | async-done | bytes 786448 | tf_op jit(solution)/shard_map/reduce_scatter | solution.py:284
  1716.2 29.7 %reduce-scatter.45.cloned.1.call-done = bf16[128,4]{1,0:T(8,128)(2,1)} async-done(((bf16[1024,4]{1,0:T(8,128)(2,1)}), bf16[128,4]{1,0:T(8,128)(2,1)}) %reduce-scatter.45.cloned.1.call-update) | async-done | bytes 1040
  1748.1 29.0 %reduce-scatter.43.cloned.1.call-done = bf16[128,4]{1,0:T(8,128)(2,1)} async-done(((bf16[1024,4]{1,0:T(8,128)(2,1)}), bf16[128,4]{1,0:T(8,128)(2,1)}) %reduce-scatter.43.cloned.1.call-update) | async-done | bytes 1040
  1777.9 9.9 all-reduce
  1788.4 132.3 %all-reduce.4.cloned.1.call-done = (bf16[1,128,3072]{2,1,0:T(8,128)(2,1)}, bf16[1,128,3072]{2,1,0:T(8,128)(2,1)}, bf16[1,128,1024]{2,1,0:T(8,128)(2,1)}, bf16[1,...) async-done(((bf16[1,128,3072]{2,1,0:T(8,128)(2,1)}, ...) | async-done | bytes 6291472 | tf_op jit(solution)/shard_map/psum | solution.py:302
  (785 shorter events, 320.3 us)
Async XLA Ops:
  7.2 70.5 %all-gather.43.cloned.1.call-start = ((), (), s32[]{:S(2)}) async-start(), calls=%async_computation.34 | async-start | bytes 7077888 | tf_op jit(solution)/shard_map/all_gather | solution.py:249
  9.9 100.5 %all-gather.37.cloned.1.call-start = ((), (), s32[]{:S(2)}) async-start(), calls=%async_computation.19 | async-start | bytes 2359296 | tf_op jit(solution)/shard_map/all_gather | solution.py:135
  23.6 58.0 %copy-start.203 = (f32[128]{0:T(128)}, f32[128]{0:T(128)S(1)}, u32[]{:S(2)}) copy-start(f32[128]{0:T(128)S(1)} %get-tuple-element.1328) | copy-start | bytes 1540
  23.6 60.5 %copy-start.201 = (f32[128]{0:T(128)}, f32[128]{0:T(128)S(1)}, u32[]{:S(2)}) copy-start(f32[128]{0:T(128)S(1)} %get-tuple-element.1327) | copy-start | bytes 1540
  23.6 57.9 %copy-start.186 = (f32[128]{0:T(128)}, f32[128]{0:T(128)S(1)}, u32[]{:S(2)}) copy-start(f32[128]{0:T(128)S(1)} %fusion.388) | copy-start | bytes 1540
  23.7 60.5 %copy-start.134 = (f32[1024,1]{0,1:T(1,128)}, f32[1024,1]{0,1:T(1,128)S(1)}, u32[]{:S(2)}) copy-start(f32[1024,1]{0,1:T(1,128)S(1)} %get-tuple-element.1613) | copy-start | bytes 12292
  23.7 230.2 %copy-start.148 = (f32[1024,1]{0,1:T(1,128)}, f32[1024,1]{0,1:T(1,128)S(1)}, u32[]{:S(2)}) copy-start(f32[1024,1]{0,1:T(1,128)S(1)} %get-tuple-element.1612) | copy-start | bytes 12292
  23.7 380.5 %copy-start.129 = (f32[1024,1]{0,1:T(1,128)}, f32[1024,1]{0,1:T(1,128)S(1)}, u32[]{:S(2)}) copy-start(f32[1024,1]{0,1:T(1,128)S(1)} %get-tuple-element.1610) | copy-start | bytes 12292
  23.7 389.6 %copy-start.150 = (f32[1024,1]{0,1:T(1,128)}, f32[1024,1]{0,1:T(1,128)S(1)}, u32[]{:S(2)}) copy-start(f32[1024,1]{0,1:T(1,128)S(1)} %get-tuple-element.1611) | copy-start | bytes 12292
  82.5 58.8 %all-gather.35.cloned.1.call-start = ((), (), s32[]{:S(2)}) async-start(), calls=%async_computation.18 | async-start | bytes 2359296 | tf_op jit(solution)/shard_map/all_gather | solution.py:136
  83.2 88.7 %all-gather.45.cloned.1.call-start = ((), (), s32[]{:S(2)}) async-start(), calls=%async_computation.35 | async-start | bytes 2359296 | tf_op jit(solution)/shard_map/all_gather | solution.py:250
  84.1 118.5 %all-gather.29.cloned.1.call-start = ((), (), s32[]{:S(2)}) async-start(), calls=%async_computation.15 | async-start | bytes 2359296 | tf_op jit(solution)/shard_map/all_gather | solution.py:135
  89.0 143.7 %all-gather.27.cloned.1.call-start = ((), (), s32[]{:S(2)}) async-start(), calls=%async_computation.14 | async-start | bytes 2359296 | tf_op jit(solution)/shard_map/all_gather | solution.py:136
  89.5 226.3 %all-gather.47.cloned.1.call-start = ((), (), s32[]{:S(2)}) async-start(), calls=%async_computation.36 | async-start | bytes 9437184 | tf_op jit(solution)/shard_map/all_gather | solution.py:251
  91.5 307.1 %all-gather.49.cloned.1.call-start = ((), (), s32[]{:S(2)}) async-start(), calls=%async_computation.37 | async-start | bytes 9437184 | tf_op jit(solution)/shard_map/all_gather | solution.py:252
  94.6 369.0 %all-gather.51.cloned.1.call-start = ((), (), s32[]{:S(2)}) async-start(), calls=%async_computation.38 | async-start | bytes 7077888 | tf_op jit(solution)/shard_map/all_gather | solution.py:249
  95.4 400.9 %all-gather.33.cloned.1.call-start = ((), (), s32[]{:S(2)}) async-start(), calls=%async_computation.17 | async-start | bytes 2359296 | tf_op jit(solution)/shard_map/all_gather | solution.py:135
  108.4 360.0 %copy-start.140 = (f32[1024,1]{0,1:T(1,128)}, f32[1024,1]{0,1:T(1,128)S(1)}, u32[]{:S(2)}) copy-start(f32[1024,1]{0,1:T(1,128)S(1)} %get-tuple-element.1609) | copy-start | bytes 12292
  156.6 52.3 %copy-start.8 = (bf16[2,512,16,64]{1,3,2,0:T(8,128)(2,1)}, bf16[2,512,16,64]{1,3,2,0:T(8,128)(2,1)S(1)}, u32[]{:S(2)}) copy-start(bf16[2,512,16,64]{1,3,2,0:T(8,128)(2,1)S(1)} %get-tuple-element.2837) | copy-start | bytes 6291460
  156.6 52.3 %copy-start.24 = (bf16[128,16,64]{0,2,1:T(8,128)(2,1)}, bf16[128,16,64]{0,2,1:T(8,128)(2,1)S(1)}, u32[]{:S(2)}) copy-start(bf16[128,16,64]{0,2,1:T(8,128)(2,1)S(1)} %get-tuple-element.2911) | copy-start | bytes 786436
  156.6 52.3 %copy-start.58 = (f32[128,16,64]{0,2,1:T(8,128)}, f32[128,16,64]{0,2,1:T(8,128)S(1)}, u32[]{:S(2)}) copy-start(f32[128,16,64]{0,2,1:T(8,128)S(1)} %get-tuple-element.579) | copy-start | bytes 1572868
  174.8 79.1 %copy-start.192 = (f32[128]{0:T(128)}, f32[128]{0:T(128)S(1)}, u32[]{:S(2)}) copy-start(f32[128]{0:T(128)S(1)} %fusion.389) | copy-start | bytes 1540
  253.4 67.2 %copy-start.194 = (f32[128]{0:T(128)}, f32[128]{0:T(128)S(1)}, u32[]{:S(2)}) copy-start(f32[128]{0:T(128)S(1)} %fusion.381) | copy-start | bytes 1540
  255.1 65.5 %copy-start.207 = (f32[128]{0:T(128)}, f32[128]{0:T(128)S(1)}, u32[]{:S(2)}) copy-start(f32[128]{0:T(128)S(1)} %get-tuple-element.1602) | copy-start | bytes 1540
  255.1 149.1 %copy-start.205 = (f32[128]{0:T(128)}, f32[128]{0:T(128)S(1)}, u32[]{:S(2)}) copy-start(f32[128]{0:T(128)S(1)} %get-tuple-element.1557) | copy-start | bytes 1540
  255.1 158.2 %copy-start.32 = (f32[128,1024]{1,0:T(8,128)}, f32[128,1024]{1,0:T(8,128)S(1)}, u32[]{:S(2)}) copy-start(f32[128,1024]{1,0:T(8,128)S(1)} %get-tuple-element.1603) | copy-start | bytes 1572868
  255.1 65.4 %copy-start.173 = (f32[128]{0:T(128)}, f32[128]{0:T(128)S(1)}, u32[]{:S(2)}) copy-start(f32[128]{0:T(128)S(1)} %fusion.390) | copy-start | bytes 1540
  320.6 83.1 %copy-start.72 = (f32[128,4096]{1,0:T(8,128)}, f32[128,4096]{1,0:T(8,128)S(1)}, u32[]{:S(2)}) copy-start(f32[128,4096]{1,0:T(8,128)S(1)} %fusion.228) | copy-start | bytes 6291460
  320.6 83.6 %copy-start.35 = (f32[128,1024]{1,0:T(8,128)S(1)}, f32[128,1024]{1,0:T(8,128)}, u32[]{:S(2)}) copy-start(f32[128,1024]{1,0:T(8,128)} %get-tuple-element.1558) | copy-start | bytes 1572868
  412.8 54.6 %copy-start.198 = (f32[128]{0:T(128)}, f32[128]{0:T(128)S(1)}, u32[]{:S(2)}) copy-start(f32[128]{0:T(128)S(1)} %fusion.383) | copy-start | bytes 1540
  413.7 53.8 %copy-start.46 = (f32[128,1024]{1,0:T(8,128)}, f32[128,1024]{1,0:T(8,128)S(1)}, u32[]{:S(2)}) copy-start(f32[128,1024]{1,0:T(8,128)S(1)} %get-tuple-element.1556) | copy-start | bytes 1572868
  413.7 54.7 %copy-start.42 = (f32[128,1024]{1,0:T(8,128)}, f32[128,1024]{1,0:T(8,128)S(1)}, u32[]{:S(2)}) copy-start(f32[128,1024]{1,0:T(8,128)S(1)} %get-tuple-element.1635) | copy-start | bytes 1572868
  413.7 59.0 %copy-start.213 = (f32[128]{0:T(128)}, f32[128]{0:T(128)S(1)}, u32[]{:S(2)}) copy-start(f32[128]{0:T(128)S(1)} %get-tuple-element.1555) | copy-start | bytes 1540
  413.7 59.0 %copy-start.215 = (f32[128]{0:T(128)}, f32[128]{0:T(128)S(1)}, u32[]{:S(2)}) copy-start(f32[128]{0:T(128)S(1)} %get-tuple-element.1634) | copy-start | bytes 1540
  468.3 58.2 %all-gather.41.cloned.1.call-start = ((), (), s32[]{:S(2)}) async-start(), calls=%async_computation.21 | async-start | bytes 2359296 | tf_op jit(solution)/shard_map/all_gather | solution.py:135
  473.6 83.0 %all-gather.39.cloned.1.call-start = ((), (), s32[]{:S(2)}) async-start(), calls=%async_computation.20 | async-start | bytes 2359296 | tf_op jit(solution)/shard_map/all_gather | solution.py:136
  474.2 113.2 %all-gather.31.cloned.1.call-start = ((), (), s32[]{:S(2)}) async-start(), calls=%async_computation.16 | async-start | bytes 2359296 | tf_op jit(solution)/shard_map/all_gather | solution.py:136
  475.0 142.5 %all-gather.53.cloned.1.call-start = ((), (), s32[]{:S(2)}) async-start(), calls=%async_computation.39 | async-start | bytes 2359296 | tf_op jit(solution)/shard_map/all_gather | solution.py:250
  475.5 225.0 %all-gather.55.cloned.1.call-start = ((), (), s32[]{:S(2)}) async-start(), calls=%async_computation.40 | async-start | bytes 9437184 | tf_op jit(solution)/shard_map/all_gather | solution.py:251
  476.1 307.1 %all-gather.57.cloned.1.call-start = ((), (), s32[]{:S(2)}) async-start(), calls=%async_computation.41 | async-start | bytes 9437184 | tf_op jit(solution)/shard_map/all_gather | solution.py:252
  476.7 442.8 %reduce-scatter.23.cloned.1.call-start = ((), (), s32[]{:S(2)}) async-start(), calls=%async_computation.24 | async-start | bytes 4718592 | tf_op jit(solution)/shard_map/reduce_scatter | solution.py:222
  620.6 79.9 %copy-start.132 = (f32[1024,1]{0,1:T(1,128)S(1)}, f32[1024,1]{0,1:T(1,128)}, u32[]{:S(2)}) copy-start(f32[1024,1]{0,1:T(1,128)} %get-tuple-element.1607) | copy-start | bytes 12292
  622.5 198.1 %copy-start.38 = (f32[128,1024]{1,0:T(8,128)}, f32[128,1024]{1,0:T(8,128)S(1)}, u32[]{:S(2)}) copy-start(f32[128,1024]{1,0:T(8,128)S(1)} %get-tuple-element.1633) | copy-start | bytes 1572868
  622.5 198.1 %copy-start.176 = (f32[128]{0:T(128)}, f32[128]{0:T(128)S(1)}, u32[]{:S(2)}) copy-start(f32[128]{0:T(128)S(1)} %fusion.394) | copy-start | bytes 1540
  853.9 116.5 %reduce-scatter.19.cloned.1.call-start = ((), (), s32[]{:S(2)}) async-start(), calls=%async_computation.22 | async-start | bytes 4718592 | tf_op jit(solution)/shard_map/reduce_scatter | solution.py:222
  876.1 275.2 %reduce-scatter.21.cloned.1.call-start = ((), (), s32[]{:S(2)}) async-start(), calls=%async_computation.23 | async-start | bytes 4718592 | tf_op jit(solution)/shard_map/reduce_scatter | solution.py:222
  879.3 91.1 %copy-start.111 = (bf16[128,1024]{1,0:T(8,128)(2,1)}, bf16[128,1024]{1,0:T(8,128)(2,1)S(1)}, u32[]{:S(2)}) copy-start(bf16[128,1024]{1,0:T(8,128)(2,1)S(1)} %copy.250) | copy-start | bytes 786436
  879.5 90.9 %copy-start.44 = (f32[128,1024]{1,0:T(8,128)S(1)}, f32[128,1024]{1,0:T(8,128)}, u32[]{:S(2)}) copy-start(f32[128,1024]{1,0:T(8,128)} %copy-done.42) | copy-start | bytes 1572868
  879.5 90.9 %copy-start.48 = (f32[128,1024]{1,0:T(8,128)S(1)}, f32[128,1024]{1,0:T(8,128)}, u32[]{:S(2)}) copy-start(f32[128,1024]{1,0:T(8,128)} %copy-done.46) | copy-start | bytes 1572868
  879.5 90.9 %copy-start.141 = (f32[1024,1]{0,1:T(1,128)S(1)}, f32[1024,1]{0,1:T(1,128)}, u32[]{:S(2)}) copy-start(f32[1024,1]{0,1:T(1,128)} %copy-done.140) | copy-start | bytes 12292
  879.6 90.9 %copy-start.179 = (f32[128]{0:T(128)S(1)}, f32[128]{0:T(128)}, u32[]{:S(2)}) copy-start(f32[128]{0:T(128)} %copy-done.178) | copy-start | bytes 1540
  879.6 90.9 %copy-start.184 = (f32[128]{0:T(128)S(1)}, f32[128]{0:T(128)}, u32[]{:S(2)}) copy-start(f32[128]{0:T(128)} %copy-done.183) | copy-start | bytes 1540
  1022.6 136.8 %reduce-scatter.25.cloned.1.call-start = ((), (), s32[]{:S(2)}) async-start(), calls=%async_computation.25 | async-start | bytes 4718592 | tf_op jit(solution)/shard_map/reduce_scatter | solution.py:222
  1049.1 132.8 %reduce-scatter.33.cloned.1.call-start = ((), (), s32[]{:S(2)}) async-start(), calls=%async_computation.29 | async-start | bytes 2359296 | tf_op jit(solution)/shard_map/reduce_scatter | solution.py:287
  1052.9 159.3 %reduce-scatter.31.cloned.1.call-start = ((), (), s32[]{:S(2)}) async-start(), calls=%async_computation.28 | async-start | bytes 2359296 | tf_op jit(solution)/shard_map/reduce_scatter | solution.py:287
  1056.8 246.1 %reduce-scatter.41.cloned.1.call-start = ((), (), s32[]{:S(2)}) async-start(), calls=%async_computation.33 | async-start | bytes 9437184 | tf_op jit(solution)/shard_map/reduce_scatter | solution.py:293
  1077.5 315.6 %reduce-scatter.37.cloned.1.call-start = ((), (), s32[]{:S(2)}) async-start(), calls=%async_computation.31 | async-start | bytes 9437184 | tf_op jit(solution)/shard_map/reduce_scatter | solution.py:290
  1099.5 364.0 %reduce-scatter.29.cloned.1.call-start = ((), (), s32[]{:S(2)}) async-start(), calls=%async_computation.27 | async-start | bytes 7077888 | tf_op jit(solution)/shard_map/reduce_scatter | solution.py:284
  1108.2 445.5 %reduce-scatter.39.cloned.1.call-start = ((), (), s32[]{:S(2)}) async-start(), calls=%async_computation.32 | async-start | bytes 9437184 | tf_op jit(solution)/shard_map/reduce_scatter | solution.py:293
  1128.7 515.1 %reduce-scatter.35.cloned.1.call-start = ((), (), s32[]{:S(2)}) async-start(), calls=%async_computation.30 | async-start | bytes 9437184 | tf_op jit(solution)/shard_map/reduce_scatter | solution.py:290
  1150.8 563.5 %reduce-scatter.27.cloned.1.call-start = ((), (), s32[]{:S(2)}) async-start(), calls=%async_computation.26 | async-start | bytes 7077888 | tf_op jit(solution)/shard_map/reduce_scatter | solution.py:284
  1168.9 577.0 %reduce-scatter.45.cloned.1.call-start = ((), (), s32[]{:S(2)}) async-start(), calls=%async_computation.43 | async-start | bytes 294912
  1170.5 606.6 %reduce-scatter.43.cloned.1.call-start = ((), (), s32[]{:S(2)}) async-start(), calls=%async_computation.42 | async-start | bytes 294912
  1181.8 738.9 %all-reduce.4.cloned.1.call-start = ((), (), s32[]{:S(2)}) async-start(), calls=%async_computation.44 | async-start | bytes 12582912 | tf_op jit(solution)/shard_map/psum | solution.py:302
  (196 other events, 1498.2 us)
Sparse Core Ops, SparseCore 0:
  10.2 67.4 all-gather.42
  82.6 27.8 all-gather.36
  112.6 28.5 all-gather.34
  143.3 28.5 all-gather.44
  174.0 28.5 all-gather.28
  204.0 28.5 all-gather.26
  234.3 81.5 all-gather.46
  318.0 80.5 all-gather.48
  400.3 63.2 all-gather.50
  468.4 27.7 all-gather.32
  497.8 28.6 all-gather.40
  528.0 28.5 all-gather.38
  558.8 28.6 all-gather.30
  588.9 28.5 all-gather.52
  618.9 81.5 all-gather.54
  702.6 80.5 all-gather.56
  854.0 65.4 reduce-scatter.22
  922.2 48.1 reduce-scatter.18
  1022.7 64.9 reduce-scatter.20
  1090.4 48.1 reduce-scatter.24
  1141.5 33.9 reduce-scatter.32
  1177.7 34.4 reduce-scatter.30
  1214.5 88.3 reduce-scatter.40
  1305.0 87.9 reduce-scatter.36
  1395.3 68.1 reduce-scatter.28
  1465.7 87.9 reduce-scatter.38
  1555.8 87.9 reduce-scatter.34
  1646.1 68.1 reduce-scatter.26
  1717.1 28.6 reduce-scatter.44
  1748.6 28.4 reduce-scatter.42
  1781.5 139.1 all-reduce.3
where the time goes:
time: 1950 us; the launch traced here: 1940 us
  waiting for transfers between devices  1370 us (70%)
  matrix products  293 us (15%)
  local copies, waits for them, and re-layouts  187 us (10%)
  blocking collectives  32.5 us (2%)
  other arithmetic  28.8 us (1%)
  between operations  20.1 us (1%)
    reduce_scatter x2, waiting for transfers between devices, body(): lax.psum_scatter(accum[3].astype(jnp.bfloat16), 'grp', scatter_dimension=...  181 us
    reduce_scatter x2, waiting for transfers between devices, body(): lax.psum_scatter(accum[2].astype(jnp.bfloat16), 'grp', scatter_dimension=...  180 us
    all_gather x2, waiting for transfers between devices, body(): lax.all_gather(w_down[layer_idx], 'grp', axis=0, tiled=True)  155 us
    reduce_scatter x2, waiting for transfers between devices, body(): lax.psum_scatter(accum[0].astype(jnp.bfloat16), 'grp', scatter_dimension=...  141 us
    all_gather x2, waiting for transfers between devices, body(): lax.all_gather(w_up[layer_idx], 'grp', axis=0, tiled=True)  139 us
    psum x1, waiting for transfers between devices, body(): lax.psum(shards[0].astype(jnp.bfloat16), 'rep').astype(jnp.float32)  132 us
    dot_general x16, matrix products, inner_rows(): lax.dot_general(left, right, (((0,), (0,)), ((), ())), preferred_element_...  110 us
    all_gather x2, waiting for transfers between devices, body(): lax.all_gather(w_qkv[layer_idx], 'grp', axis=0, tiled=True)  104 us
  transfers between devices with their start and end apart: 31, of which 28 were waited for; matrix products, arithmetic and copies ran while one was open for 18% of the time, Pallas kernels for 0%

commit v1 on v0

--- a/solution.py
+++ b/solution.py
@@ -1,14 +1,330 @@
+import functools
+
 import jax
 import jax.numpy as jnp
 from jax import lax
+from jax.experimental import pallas as pl
+from jax.experimental.pallas import tpu as pltpu
 from jax.sharding import PartitionSpec as P
 
 HEADS = 16
 HDIM = 64
-
-
 EPS = 1e-06
 NEGATIVE = -1e30
+BF = jnp.bfloat16
+F32 = jnp.float32
+
+
+def flip(axis, bit, value):
+    size = lax.axis_size(axis)
+    return lax.ppermute(value, axis, [(i, i ^ bit) for i in range(size)])
+
+
+core = functools.partial(flip, "grp", 1)
+near = functools.partial(flip, "grp", 2)
+far = functools.partial(flip, "grp", 4)
+along_x = functools.partial(flip, "rep", 1)
+along_y = functools.partial(flip, "rep", 2)
+
+
+def pick(stacked, index):
+    return lax.dynamic_index_in_dim(stacked, index, 0, keepdims=False)
+
+
+def dot(left, right):
+    return jnp.dot(left, right, preferred_element_type=F32)
+
+
+def dot_tn(left, right):
+    return lax.dot_general(left, right, (((0,), (0,)), ((), ())), preferred_element_type=F32)
+
+
+def dot_nt(left, right):
+    return lax.dot_general(left, right, (((1,), (1,)), ((), ())), preferred_element_type=F32)
+
+
+def norm(values, gain):
+    return values * lax.rsqrt(jnp.mean(values * values, axis=-1, keepdims=True) + EPS) * gain
+
+
+def norm_back(values, gain, grad):
+    rstd = lax.rsqrt(jnp.mean(values * values, axis=-1, keepdims=True) + EPS)
+    hat = values * rstd
+    scaled = grad * gain
+    back = rstd * (scaled - hat * jnp.mean(scaled * hat, axis=-1, keepdims=True))
+    return back, jnp.sum(grad * hat, axis=0)
+
+
+def head_mask(width, head):
+    lanes = lax.broadcasted_iota(jnp.int32, (1, width), 1)
+    return (lanes // HDIM) == head
+
+
+def attend_kernel(block, qkv_ref, mixed_ref, lse_ref):
+    length, width = mixed_ref.shape
+    heads = width // HDIM
+    row = lax.broadcasted_iota(jnp.int32, (block, block), 0)
+    col = lax.broadcasted_iota(jnp.int32, (block, block), 1)
+    below = col <= row
+    zero = jnp.zeros((), BF)
+    lane = lax.broadcasted_iota(jnp.int32, (1, 128), 1)
+    for start in range(0, length, block):
+        stop = start + block
+        query = qkv_ref[start:stop, :width] * jnp.asarray(HDIM**-0.5, BF)
+        total = jnp.zeros((block, width), F32)
+        stats = jnp.zeros((block, 128), F32)
+        for head in range(heads):
+            mask = head_mask(width, head)
+            keys = jnp.where(mask, qkv_ref[:stop, width : 2 * width], zero)
+            vals = jnp.where(mask, qkv_ref[:stop, 2 * width :], zero)
+            scores = dot_nt(query, keys)
+            last = jnp.where(below, scores[:, start:], NEGATIVE)
+            scores = jnp.concatenate([scores[:, :start], last], axis=1) if start else last
+            top = jnp.max(scores, axis=1, keepdims=True)
+            terms = jnp.exp(scores - top)
+            sums = jnp.sum(terms, axis=1, keepdims=True)
+            total = total + dot(terms.astype(BF), vals) * (1.0 / sums)
+            stats = jnp.where(lane == head, top + jnp.log(sums), stats)
+        mixed_ref[start:stop, :] = total.astype(BF)
+        lse_ref[start:stop, :] = stats
+
+
+def attend(qkv):
+    length, width = qkv.shape[0], qkv.shape[1] // 3
+    heads = width // HDIM
+    return pl.pallas_call(
+        functools.partial(attend_kernel, 256),
+        out_shape=(
+            jax.ShapeDtypeStruct((length, width), BF),
+            jax.ShapeDtypeStruct((length, 128), F32),
+        ),
+        compiler_params=pltpu.CompilerParams(vmem_limit_bytes=40 << 20),
+        cost_estimate=pl.CostEstimate(
+            flops=8 * heads * length * length * HDIM,
+            bytes_accessed=length * width * 8 + length * 512,
+            transcendentals=heads * length * length // 2,
+        ),
+    )(qkv)
+
+
+def attend_back_kernel(block, qkv_ref, lse_ref, grad_ref, out_ref, dk_ref, dv_ref):
+    length, width = grad_ref.shape
+    heads = width // HDIM
+    row = lax.broadcasted_iota(jnp.int32, (block, block), 0)
+    col = lax.broadcasted_iota(jnp.int32, (block, block), 1)
+    below = col <= row
+    zero = jnp.zeros((), BF)
+    scale = HDIM**-0.5
+    dk_ref[...] = jnp.zeros_like(dk_ref)
+    dv_ref[...] = jnp.zeros_like(dv_ref)
+    for start in range(0, length, block):
+        stop = start + block
+        query = qkv_ref[start:stop, :width] * jnp.asarray(scale, BF)
+        grad = grad_ref[start:stop, :]
+        dq = jnp.zeros((block, width), F32)
+        for head in range(heads):
+            mask = head_mask(width, head)
+            keys = jnp.where(mask, qkv_ref[:stop, width : 2 * width], zero)
+            vals = jnp.where(mask, qkv_ref[:stop, 2 * width :], zero)
+            scores = dot_nt(query, keys)
+            last = jnp.where(below, scores[:, start:], NEGATIVE)
+            scores = jnp.concatenate([scores[:, :start], last], axis=1) if start else last
+            probs = jnp.exp(scores - lse_ref[start:stop, head : head + 1])
+            prob_grad = dot_nt(grad, vals)
+            delta = jnp.sum(probs * prob_grad, axis=1, keepdims=True)
+            score_grad = (probs * (prob_grad - delta)).astype(BF)
+            dq = dq + dot(score_grad, keys)
+            dk_ref[:stop, :] += dot_tn(score_grad, jnp.where(mask, query, zero))
+            dv_ref[:stop, :] += dot_tn(probs.astype(BF), jnp.where(mask, grad, zero))
+        out_ref[start:stop, :width] = (dq * scale).astype(BF)
+    out_ref[:, width : 2 * width] = dk_ref[...].astype(BF)
+    out_ref[:, 2 * width :] = dv_ref[...].astype(BF)
+
+
+def attend_back(qkv, lse, grad):
+    length, width = grad.shape
+    heads = width // HDIM
+    return pl.pallas_call(
+        functools.partial(attend_back_kernel, 256),
+        out_shape=jax.ShapeDtypeStruct((length, 3 * width), BF),
+        scratch_shapes=[pltpu.VMEM((length, width), F32)] * 2,
+        compiler_params=pltpu.CompilerParams(vmem_limit_bytes=40 << 20),
+        cost_estimate=pl.CostEstimate(
+            flops=20 * heads * length * length * HDIM,
+            bytes_accessed=length * width * 14 + length * 512,
+            transcendentals=heads * length * length // 2,
+        ),
+    )(qkv, lse, grad)
+
+
+def gather4(mine, place):
+    other = core(mine)
+    across = near(mine)
+    corner = core(across)
+    halves, rows, width = mine.shape
+    whole = jnp.zeros((halves, 4, rows, width), mine.dtype)
+    for value, where in ((mine, place), (other, place ^ 1), (across, place ^ 2), (corner, place ^ 3)):
+        whole = lax.dynamic_update_slice(whole, value[:, None], (0, where, 0, 0))
+    return whole.reshape(halves * 4 * rows, width)
+
+
+def scatter4(part, place):
+    total, width = part.shape
+    part = part.reshape(2, 4, total // 8, width)
+
+    def term(where):
+        return lax.dynamic_slice(part, (0, where, 0, 0), (2, 1, total // 8, width))[:, 0]
+
+    across = core(term(place ^ 3).astype(BF)).astype(F32) + term(place ^ 2)
+    across = near(across.astype(BF))
+    mine = core(term(place ^ 1).astype(BF)).astype(F32) + term(place)
+    return (mine + across.astype(F32)).reshape(total // 4, width)
+
+
+def spread_rep(mine, rep):
+    return lax.all_gather(mine, "rep", axis=0, tiled=False)
+
+
+def columns_in(weight, groups, unit, rep, place):
+    rows, total = weight.shape
+    quarter = pick(weight.reshape(4, rows // 4, total), rep)
+    whole = lax.all_gather(quarter, "grp", axis=0, tiled=False)
+    whole = whole.reshape(8, rows // 4, groups, 4, unit)
+    mine = lax.dynamic_index_in_dim(whole, place, 3, keepdims=False)
+    mine = mine.reshape(8, rows // 4, groups * unit)
+    return lax.all_gather(mine, "rep", axis=1, tiled=True).reshape(8 * rows, groups * unit)
+
+
+def columns_out(grad, groups, unit, rep, place, upper):
+    total, width = grad.shape
+    rows = total // 32
+    low = grad.reshape(8, 4, rows, width)
+    mine = lax.psum_scatter(low, "rep", scatter_dimension=1, tiled=False)
+    mine = mine.reshape(2, 4, rows, width)
+    other = far(pick(mine, 1 - upper))
+    mine = (pick(mine, upper).astype(F32) + other.astype(F32)).astype(BF)
+    side = place // 2
+    mine = mine.reshape(2, 2, rows, width)
+    other = near(pick(mine, 1 - side))
+    mine = pick(mine, side)
+    mine = jnp.where(side == 0, jnp.stack([mine, other]), jnp.stack([other, mine]))
+    which = place % 2
+    keep = lax.dynamic_index_in_dim(mine, which, 1, keepdims=False)
+    give = lax.dynamic_index_in_dim(mine, 1 - which, 1, keepdims=False)
+    other = core(give)
+    both = jnp.where(which == 0, jnp.stack([keep, other], 1), jnp.stack([other, keep], 1))
+    both = both.reshape(4, rows, groups, unit).transpose(1, 2, 0, 3).reshape(rows, groups * 4 * unit)
+    return lax.all_gather(both, "rep", axis=0, tiled=True).astype(F32)
+
+
+def rows_in(weight, upper):
+    other = far(weight)
+    return jnp.where(
+        upper == 0, jnp.concatenate([weight, other]), jnp.concatenate([other, weight])
+    )
+
+
+def rows_out(grad, rep, upper):
+    total, width = grad.shape
+    rows = total // 8
+    low = grad.reshape(2, 4, rows, width)
+    mine = lax.psum_scatter(low, "rep", scatter_dimension=1, tiled=False)
+    other = far(pick(mine, 1 - upper))
+    mine = (pick(mine, upper).astype(F32) + other.astype(F32)).astype(BF)
+    return lax.all_gather(mine, "rep", axis=0, tiled=True).astype(F32)
+
+
+def body_pairs(block_in, cotangent, w_qkv, w_out, w_up, w_down, norm_gains):
+    layers, rows, width = w_out.shape
+    tokens = block_in.shape[2]
+    hidden_unit = w_down.shape[1]
+    rep = lax.axis_index("rep")
+    grp = lax.axis_index("grp")
+    place, upper = grp % 4, grp // 4
+
+    gains = lax.all_gather(norm_gains, "grp", axis=1, tiled=True).astype(F32)
+    gains = jnp.transpose(gains, (0, 2, 1))
+
+    def bring(two):
+        mine = pick(two[:, 0], upper)
+        other = far(pick(two[:, 0], 1 - upper))
+        return jnp.where(upper == 0, jnp.stack([mine, other]), jnp.stack([other, mine])).astype(F32)
+
+    def send_back(mine):
+        keep = pick(mine, upper)
+        other = far(pick(mine, 1 - upper))
+        return jnp.where(upper == 0, jnp.stack([keep, other]), jnp.stack([other, keep]))
+
+    hidden = bring(block_in).reshape(2 * tokens, width)
+    weights = []
+    for layer in range(layers):
+        weights.append(
+            (
+                columns_in(w_qkv[layer], 6, rows, rep, place),
+                rows_in(w_out[layer], upper),
+                columns_in(w_up[layer], 2, hidden_unit, rep, place),
+                rows_in(w_down[layer], upper),
+            )
+        )
+
+    def gather(values):
+        return gather4(values.reshape(2, tokens, width), place)
+
+    saved = []
+    for layer in range(layers):
+        qkv_w, out_w, up_w, down_w = weights[layer]
+        gain = gains[layer]
+        normed = gather(norm(hidden, gain[0]).astype(BF))
+        qkv = dot(normed, qkv_w).astype(BF)
+        mixed, lse = attend(qkv)
+        attn_out = scatter4(dot(mixed, out_w), place)
+        resid = hidden + norm(attn_out, gain[1])
+        mlp_in = gather(norm(resid, gain[2]).astype(BF))
+        up_out = dot(mlp_in, up_w)
+        active = jax.nn.gelu(up_out).astype(BF)
+        down_out = scatter4(dot(active, down_w), place)
+        saved.append((hidden, normed, qkv, mixed, lse, attn_out, resid, mlp_in, up_out, active, down_out))
+        hidden = resid + norm(down_out, gain[3])
+    block_out = send_back(hidden.astype(BF).reshape(2, tokens, width))[:, None]
+
+    grad = bring(cotangent).reshape(2 * tokens, width)
+    results = [None] * layers
+    gain_grads = [None] * layers
+    for layer in reversed(range(layers)):
+        qkv_w, out_w, up_w, down_w = weights[layer]
+        gain = gains[layer]
+        hidden, normed, qkv, mixed, lse, attn_out, resid, mlp_in, up_out, active, down_out = saved[layer]
+        down_grad, four = norm_back(down_out, gain[3], grad)
+        down_low = gather(down_grad.astype(BF))
+        down_w_grad = dot_tn(active, down_low).astype(BF)
+        active_grad = dot_nt(down_low, down_w)
+        unused, puller = jax.vjp(jax.nn.gelu, up_out)
+        up_low = puller(active_grad)[0].astype(BF)
+        up_w_grad = dot_tn(mlp_in, up_low).astype(BF)
+        mlp_grad = scatter4(dot_nt(up_low, up_w), place)
+        part, three = norm_back(resid, gain[2], mlp_grad)
+        resid_grad = grad + part
+        attn_grad, two = norm_back(attn_out, gain[1], resid_grad)
+        attn_low = gather(attn_grad.astype(BF))
+        out_w_grad = dot_tn(mixed, attn_low).astype(BF)
+        mixed_grad = dot_nt(attn_low, out_w).astype(BF)
+        qkv_grad = attend_back(qkv, lse, mixed_grad)
+        qkv_w_grad = dot_tn(normed, qkv_grad).astype(BF)
+        normed_grad = scatter4(dot_nt(qkv_grad, qkv_w), place)
+        part, one = norm_back(hidden, gain[0], normed_grad)
+        grad = resid_grad + part
+        gain_grads[layer] = jnp.stack([one, two, three, four], axis=1)
+        results[layer] = (
+            columns_out(qkv_w_grad, 6, rows, rep, place, upper),
+            rows_out(out_w_grad, rep, upper),
+            columns_out(up_w_grad, 2, hidden_unit, rep, place, upper),
+            rows_out(down_w_grad, rep, upper),
+        )
+    block_in_grad = send_back(grad.astype(BF).reshape(2, tokens, width)).astype(F32)[:, None]
+    gain_all = lax.psum(jnp.stack(gain_grads), ("rep", "grp"))
+    gain_mine = lax.dynamic_slice_in_dim(gain_all, grp * rows, rows, 1)
+    stacked = [jnp.stack([results[layer][k] for layer in range(layers)]) for k in range(4)]
+    return (block_out, block_in_grad, *stacked, gain_mine)
 
 
 def norm_apply(values, gains):
@@ -48,7 +364,7 @@
     return (scores, allowed[None])
 
 
-def attend(query, keys_all, values_all, query_pos):
+def attend_split(query, keys_all, values_all, query_pos):
     key_blocks, width, count = split_blocks(keys_all)
     value_blocks = split_blocks(values_all)[0]
     row_count = query.shape[0]
@@ -82,7 +398,7 @@
     return (mixed.reshape(row_count, HEADS * HDIM), log_total)
 
 
-def attend_back(query, keys_all, values_all, log_total, out_grad, delta, query_pos):
+def attend_back_split(query, keys_all, values_all, log_total, out_grad, delta, query_pos):
     key_blocks, width, count = split_blocks(keys_all)
     value_blocks = split_blocks(values_all)[0]
     row_count = query.shape[0]
@@ -135,7 +451,7 @@
         lax.all_gather(qkv_low[:, width : 2 * width], "grp", axis=0, tiled=True),
         lax.all_gather(qkv_low[:, 2 * width :], "grp", axis=0, tiled=True),
     )
-    mixed, log_total = attend(
+    mixed, log_total = attend_split(
         query.reshape(row_count, HEADS, HDIM),
         keys_all.reshape(-1, HEADS, HDIM),
         values_all.reshape(-1, HEADS, HDIM),
@@ -210,7 +526,7 @@
         (mixed_grad.astype(jnp.float32) * mixed).reshape(row_count, HEADS, HDIM), axis=-1
     ).T
     query_low = qkv_low[:, :width]
-    query_grad, key_value_terms = attend_back(
+    query_grad, key_value_terms = attend_back_split(
         query_low.reshape(row_count, HEADS, HDIM),
         keys_all.reshape(-1, HEADS, HDIM),
         values_all.reshape(-1, HEADS, HDIM),
@@ -231,7 +547,7 @@
     return (resid_grad + input_part, (w_qkv_grad, w_out_grad, w_up_grad, w_down_grad, gain_grad))
 
 
-def body(block_in, cotangent, w_qkv, w_out, w_up, w_down, norm_gains):
+def body_general(block_in, cotangent, w_qkv, w_out, w_up, w_down, norm_gains):
     layer_count = w_qkv.shape[0]
     micro_count = block_in.shape[0]
     row_count = block_in.shape[2]
@@ -316,26 +632,19 @@
 
 
 def solution(mesh):
+    rep_size, grp_size = mesh.shape["rep"], mesh.shape["grp"]
+
+    def body(block_in, cotangent, w_qkv, w_out, w_up, w_down, norm_gains):
+        fits = (rep_size, grp_size, block_in.shape[0]) == (4, 8, 2)
+        chosen = body_pairs if fits else body_general
+        return chosen(block_in, cotangent, w_qkv, w_out, w_up, w_down, norm_gains)
+
+    tokens = P(None, "rep", "grp", None)
+    rows = P(None, "grp", None)
     return jax.shard_map(
         body,
         mesh=mesh,
-        in_specs=(
-            P(None, "rep", "grp", None),
-            P(None, "rep", "grp", None),
-            P(None, "grp", None),
-            P(None, "grp", None),
-            P(None, "grp", None),
-            P(None, "grp", None),
-            P(None, "grp", None),
-        ),
-        out_specs=(
-            P(None, "rep", "grp", None),
-            P(None, "rep", "grp", None),
-            P(None, "grp", None),
-            P(None, "grp", None),
-            P(None, "grp", None),
-            P(None, "grp", None),
-            P(None, "grp", None),
-        ),
+        in_specs=(tokens, tokens, rows, rows, rows, rows, rows),
+        out_specs=(tokens, tokens, rows, rows, rows, rows, rows),
         check_vma=False,
     )

time: 1950 us -> 1040 us (0.53)
  waiting for transfers between devices: 1370 us -> 596 us
  matrix products: 293 us -> 87.6 us
  local copies, waits for them, and re-layouts: 187 us -> 98.8 us
  blocking collectives: 32.5 us -> 104 us
  starting transfers between devices: 2.3 us -> 55.7 us
  Pallas kernels: 0 us -> 30.9 us
    reduce_scatter x12 -> x0, waiting for transfers between devices: 617 us -> none  [the longest x2 181 us: body(): lax.psum_scatter(accum[3].astype(jnp.bfloat16), 'grp', scatter_dimension=...]
    all_gather x16 -> x12, waiting for transfers between devices: 557 us -> 37.5 us  [the longest x4 25.9 us: columns_in(): whole = lax.all_gather(quarter, 'grp', axis=0, tiled=False)]
    ppermute x0 -> x72, waiting for transfers between devices: none -> 338 us  [flip(): return lax.ppermute(value, axis, [(i, i ^ bit) for i in range(size)])]
    dot_general x76 -> x24, matrix products: 293 us -> 87.6 us  [the longest x8 31.4 us: dot_tn(): lax.dot_general(left, right, (((0,), (0,)), ((), ())), preferred_element_...]
    unnamed x33 -> x14, waiting for transfers between devices: 63.7 us -> 220 us
    psum x1 -> x0, waiting for transfers between devices: 132 us -> none  [body(): lax.psum(shards[0].astype(jnp.bfloat16), 'rep').astype(jnp.float32)]
    unnamed x434 -> x105, local copies, waits for them, and re-layouts: 69.6 us -> 12.2 us
    another operation x28 -> x10, local copies, waits for them, and re-layouts: 62.1 us -> 7.58 us  [the longest x8 50.8 us: split_blocks(): return (whole.reshape(count, width, HEADS, HDIM), width, count)]
  transfers between devices with their start and end apart: 31 -> 85, of which waited for: 28 -> 41; matrix products, arithmetic and copies ran while one was open for 18% -> 16% of each run, Pallas kernels for 0% -> 1%
where the time goes in v1:
time: 1040 us; the launch traced here: 1030 us
  waiting for transfers between devices  596 us (57%)
  blocking collectives  104 us (10%)
  local copies, waits for them, and re-layouts  98.8 us (10%)
  matrix products  87.6 us (8%)
  starting transfers between devices  55.7 us (5%)
  other arithmetic  42.7 us (4%)
  Pallas kernels  30.9 us (3%)
  between operations  16.3 us (2%)
    ppermute x72, waiting for transfers between devices, flip(): return lax.ppermute(value, axis, [(i, i ^ bit) for i in range(size)])  338 us
    unnamed x14, waiting for transfers between devices  220 us
    ppermute x72, starting transfers between devices, flip(): return lax.ppermute(value, axis, [(i, i ^ bit) for i in range(size)])  54.1 us
    psum x1, blocking collectives, body_pairs(): gain_all = lax.psum(jnp.stack(gain_grads), ('rep', 'grp'))  41.7 us
    dot_general x8, matrix products, dot_tn(): lax.dot_general(left, right, (((0,), (0,)), ((), ())), preferred_element_...  31.4 us
    dot_general x8, matrix products, dot(): return jnp.dot(left, right, preferred_element_type=F32)  30.7 us
    all_gather x4, waiting for transfers between devices, columns_in(): whole = lax.all_gather(quarter, 'grp', axis=0, tiled=False)  25.9 us
    dot_general x8, matrix products, dot_nt(): lax.dot_general(left, right, (((1,), (1,)), ((), ())), preferred_element_...  25.4 us
  transfers between devices with their start and end apart: 85, of which 41 were waited for; matrix products, arithmetic and copies ran while one was open for 16% of the time, Pallas kernels for 1%

profile of v1, /device:TPU:0, one launch (start us, length us, event | category | flops | bytes accessed | tf_op | source)
XLA Modules:
  0.0 1031.8 jit_solution(10462989959465845084)
XLA Ops:
  13.4 25.9 %all-gather.13.cloned.1.call-done = bf16[8,32,3072]{2,1,0:T(8,128)(2,1)} async-done(((bf16[1,32,3072]{2,1,0:T(8,128)(2,1)}), bf16[8,32,3072]{2,1,0:T(8,128)(2,1)}) %all-gather.13.cloned.1.call-update) | async-done | bytes 1572880 | tf_op jit(solution)/shard_map/all_gather | solution.py:191
  39.3 3.2 reshape.2355
  49.1 18.7 %all_gather.55 = bf16[2,1024,4]{1,2,0:T(4,128)(2,1)S(1)} all-gather(bf16[2,128,4]{1,2,0:T(4,128)(2,1)S(1)} %copy-done.43), channel_id=1, replica_groups=mesh['rep'=4,'grp'=8] {'grp'}, dimensions={1}, use_global_device_ids=true | all-gather | bytes 18432 | tf_op jit(solution)/shard_map/all_gather | solution.py:245
  67.9 7.0 collective-permute-done
  79.5 3.5 collective-permute-start.4
  83.0 13.2 %collective-permute-done.2 = bf16[2,128,1024]{2,1,0:T(8,128)(2,1)S(1)} collective-permute-done((bf16[2,128,1024]{2,1,0:T(8,128)(2,1)S(1)}, bf16[2,128,1024]{2,1,0:T(8,128)(2,1)S(1)}, u32[]{:S(2)}, u32[]{:S(2)}) %collective-permute-start.2) | collective-permute-done | bytes 524320 | tf_op jit(solution)/shard_map/ppermute | solution.py:20
  101.5 4.8 reshape.2360
  106.2 7.6 all-gather.15.cloned.1.call-done
  113.9 3.8 convolution_convert_fusion.7.qkv_ref
  117.7 4.7 shard_map.126
  126.6 3.6 dynamic-slice_reduce_fusion.1
  135.5 14.5 %collective-permute-done.7 = bf16[2,128,1024]{2,1,0:T(8,128)(2,1)S(1)} collective-permute-done((bf16[2,128,1024]{2,1,0:T(8,128)(2,1)S(1)}, bf16[2,128,1024]{2,1,0:T(8,128)(2,1)S(1)}, u32[]{:S(2)}, u32[]{:S(2)}) %collective-permute-start.7) | collective-permute-done | bytes 524320 | tf_op jit(solution)/shard_map/ppermute | solution.py:20
  159.6 4.2 reshape.2365
  163.8 15.1 %collective-permute-done.9 = bf16[2,128,1024]{2,1,0:T(8,128)(2,1)} collective-permute-done((bf16[2,128,1024]{2,1,0:T(8,128)(2,1)}, bf16[2,128,1024]{2,1,0:T(8,128)(2,1)}, u32[]{:S(2)}, u32[]{:S(2)}) %collective-permute-start.9) | collective-permute-done | bytes 524320 | tf_op jit(solution)/shard_map/ppermute | solution.py:20
  178.9 4.6 dynamic-slice_reduce_fusion.2
  191.6 4.7 fusion.100
  196.3 10.4 %collective-permute-done.11 = bf16[512,1024]{1,0:T(8,128)(2,1)} collective-permute-done((bf16[512,1024]{1,0:T(8,128)(2,1)}, bf16[512,1024]{1,0:T(8,128)(2,1)}, u32[]{:S(2)}, u32[]{:S(2)}) %collective-permute-start.11) | collective-permute-done | bytes 1048608 | tf_op jit(solution)/shard_map/ppermute | solution.py:20
  206.7 5.7 fusion.75
  219.3 15.6 %collective-permute-done.14 = bf16[2,128,1024]{2,1,0:T(8,128)(2,1)} collective-permute-done((bf16[2,128,1024]{2,1,0:T(8,128)(2,1)}, bf16[2,128,1024]{2,1,0:T(8,128)(2,1)}, u32[]{:S(2)}, u32[]{:S(2)}) %collective-permute-start.14) | collective-permute-done | bytes 524320 | tf_op jit(solution)/shard_map/ppermute | solution.py:20
  240.3 19.0 %collective-permute-done.16 = bf16[2,128,1024]{2,1,0:T(8,128)(2,1)S(1)} collective-permute-done((bf16[2,128,1024]{2,1,0:T(8,128)(2,1)S(1)}, bf16[2,128,1024]{2,1,0:T(8,128)(2,1)S(1)}, u32[]{:S(2)}, u32[]{:S(2)}) %collective-permute-start.16) | collective-permute-done | bytes 524320 | tf_op jit(solution)/shard_map/ppermute | solution.py:20
  264.7 3.8 convolution_convert_fusion.6.qkv_ref
  268.5 4.7 shard_map.127
  279.8 4.5 reshape.2370
  284.3 6.0 dynamic-slice_reduce_fusion
  295.3 13.7 %collective-permute-done.21 = bf16[2,128,1024]{2,1,0:T(8,128)(2,1)S(1)} collective-permute-done((bf16[2,128,1024]{2,1,0:T(8,128)(2,1)S(1)}, bf16[2,128,1024]{2,1,0:T(8,128)(2,1)S(1)}, u32[]{:S(2)}, u32[]{:S(2)}) %collective-permute-start.21) | collective-permute-done | bytes 524320 | tf_op jit(solution)/shard_map/ppermute | solution.py:20
  313.9 12.8 %collective-permute-done.23 = bf16[2,128,1024]{2,1,0:T(8,128)(2,1)S(1)} collective-permute-done((bf16[2,128,1024]{2,1,0:T(8,128)(2,1)S(1)}, bf16[2,128,1024]{2,1,0:T(8,128)(2,1)S(1)}, u32[]{:S(2)}, u32[]{:S(2)}) %collective-permute-start.23) | collective-permute-done | bytes 524320 | tf_op jit(solution)/shard_map/ppermute | solution.py:20
  331.2 4.5 fusion.101
  335.8 40.2 %collective-permute-done.25 = bf16[512,1024]{1,0:T(8,128)(2,1)} collective-permute-done((bf16[512,1024]{1,0:T(8,128)(2,1)}, bf16[512,1024]{1,0:T(8,128)(2,1)}, u32[]{:S(2)}, u32[]{:S(2)}) %collective-permute-start.25) | collective-permute-done | bytes 1048608 | tf_op jit(solution)/shard_map/ppermute | solution.py:20
  375.9 5.7 fusion.73
  384.1 3.4 collective-permute-start.30
  387.6 16.0 %collective-permute-done.28 = bf16[2,128,1024]{2,1,0:T(8,128)(2,1)S(1)} collective-permute-done((bf16[2,128,1024]{2,1,0:T(8,128)(2,1)S(1)}, bf16[2,128,1024]{2,1,0:T(8,128)(2,1)S(1)}, u32[]{:S(2)}, u32[]{:S(2)}) %collective-permute-start.28) | collective-permute-done | bytes 524320 | tf_op jit(solution)/shard_map/ppermute | solution.py:20
  407.2 11.7 %collective-permute-done.32 = bf16[2,128,1024]{2,1,0:T(8,128)(2,1)S(1)} collective-permute-done((bf16[2,128,1024]{2,1,0:T(8,128)(2,1)S(1)}, bf16[2,128,1024]{2,1,0:T(8,128)(2,1)S(1)}, u32[]{:S(2)}, u32[]{:S(2)}) %collective-permute-start.32) | collective-permute-done | bytes 524320 | tf_op jit(solution)/shard_map/ppermute | solution.py:20
  420.9 7.1 fusion.13
  434.5 12.2 %collective-permute-done.36 = bf16[2,128,1024]{2,1,0:T(8,128)(2,1)S(1)} collective-permute-done((bf16[2,128,1024]{2,1,0:T(8,128)(2,1)S(1)}, bf16[2,128,1024]{2,1,0:T(8,128)(2,1)S(1)}, u32[]{:S(2)}, u32[]{:S(2)}) %collective-permute-start.36) | collective-permute-done | bytes 524320 | tf_op jit(solution)/shard_map/ppermute | solution.py:20
  450.3 11.4 %collective-permute-done.38 = bf16[2,128,1024]{2,1,0:T(8,128)(2,1)S(1)} collective-permute-done((bf16[2,128,1024]{2,1,0:T(8,128)(2,1)S(1)}, bf16[2,128,1024]{2,1,0:T(8,128)(2,1)S(1)}, u32[]{:S(2)}, u32[]{:S(2)}) %collective-permute-start.38) | collective-permute-done | bytes 524320 | tf_op jit(solution)/shard_map/ppermute | solution.py:20
  465.6 10.8 %shard_map.128 = bf16[1024,768]{1,0:T(8,128)(2,1)S(1)} custom-call(bf16[1024,768]{1,0:T(8,128)(2,1)S(1)} %copy-done.1, f32[1024,128]{1,0:T(8,128)S(1)} %get-tuple-element.13.lse_ref, bf16[1024,256]{1,0:T(8,128)(2,1)S(1)} %convolution_convert_fusion.11.grad_ref), custom_call_target="tpu_custom_call" | custom-call | flops 5368709120 | bytes 4194304 | tf_op jit(solution)/shard_map/pallas_call | solution.py:147
  482.3 12.2 %collective-permute-done.42 = bf16[2,128,1024]{2,1,0:T(8,128)(2,1)S(1)} collective-permute-done((bf16[2,128,1024]{2,1,0:T(8,128)(2,1)S(1)}, bf16[2,128,1024]{2,1,0:T(8,128)(2,1)S(1)}, u32[]{:S(2)}, u32[]{:S(2)}) %collective-permute-start.42) | collective-permute-done | bytes 524320 | tf_op jit(solution)/shard_map/ppermute | solution.py:20
  498.0 11.4 %collective-permute-done.44 = bf16[2,128,1024]{2,1,0:T(8,128)(2,1)S(1)} collective-permute-done((bf16[2,128,1024]{2,1,0:T(8,128)(2,1)S(1)}, bf16[2,128,1024]{2,1,0:T(8,128)(2,1)S(1)}, u32[]{:S(2)}, u32[]{:S(2)}) %collective-permute-start.44) | collective-permute-done | bytes 524320 | tf_op jit(solution)/shard_map/ppermute | solution.py:20
  509.5 4.1 convolution_convert_fusion
  513.7 7.3 fusion.6
  524.1 5.3 convolution_convert_fusion.2
  532.9 4.7 convolution_convert_fusion.4
  537.7 6.3 collective-permute-done.48
  547.9 4.3 convolution_convert_fusion.1
  552.2 7.5 collective-permute-done.50
  559.7 5.3 convolution_convert_fusion.3
  567.8 10.7 %shard_map.129 = bf16[1024,768]{1,0:T(8,128)(2,1)S(1)} custom-call(bf16[1024,768]{1,0:T(8,128)(2,1)S(1)} %convolution_convert_fusion.7.qkv_ref, f32[1024,128]{1,0:T(8,128)S(1)} %copy-done.3, bf16[1024,256]{1,0:T(8,128)(2,1)S(1)} %convolution_convert_fusion.10.grad_ref), custom_call_target="tpu_custom_call" | custom-call | flops 5368709120 | bytes 4194304 | tf_op jit(solution)/shard_map/pallas_call | solution.py:147
  578.5 4.6 convolution_convert_fusion.5
  593.7 14.4 %collective-permute-done.29 = bf16[128,1024]{1,0:T(8,128)(2,1)S(1)} collective-permute-done((bf16[128,1024]{1,0:T(8,128)(2,1)S(1)}, bf16[128,1024]{1,0:T(8,128)(2,1)S(1)}, u32[]{:S(2)}, u32[]{:S(2)}) %collective-permute-start.29) | collective-permute-done | bytes 262176 | tf_op jit(solution)/shard_map/ppermute | solution.py:20
  608.9 219.6 %all-reduce.11.cloned.1.call-done = (bf16[8,4,32,768]{3,2,1,0:T(8,128)(2,1)}, bf16[8,4,32,768]{3,2,1,0:T(8,128)(2,1)}, bf16[2,4,32,1024]{3,2,1,0:T(8,128)(2,1)},...) async-done(((bf16[8,4,32,768]{3,2,1,0:T(8,128)(2,1)}, ...) | async-done | bytes 12582928
  833.9 10.2 collective-permute-done.70
  846.4 41.7 %psum.7 = f32[2,1024,4]{1,2,0:T(4,128)S(1)} all-reduce(f32[2,1024,4]{1,2,0:T(4,128)S(1)} %pad_maximum_fusion), channel_id=1, replica_groups=mesh['rep'=4,'grp'=8] {'rep','grp'}, use_global_device_ids=true, to_apply=%region_32.33 | all-reduce | flops 8192 | bytes 65536 | tf_op jit(solution)/shard_map/psum | solution.py:324
  892.8 2.9 collective-permute-start.64
  897.3 2.9 collective-permute-start.62
  901.7 16.4 %collective-permute-done.71 = bf16[128,1024]{1,0:T(8,128)(2,1)S(1)} collective-permute-done((bf16[128,1024]{1,0:T(8,128)(2,1)S(1)}, bf16[128,1024]{1,0:T(8,128)(2,1)S(1)}, u32[]{:S(2)}, u32[]{:S(2)}) %collective-permute-start.71) | collective-permute-done | bytes 262176 | tf_op jit(solution)/shard_map/ppermute | solution.py:20
  924.9 14.3 %collective-permute-done.62 = bf16[32,1024]{1,0:T(8,128)(2,1)S(1)} collective-permute-done((bf16[32,1024]{1,0:T(8,128)(2,1)}, bf16[32,1024]{1,0:T(8,128)(2,1)S(1)}, u32[]{:S(2)}, u32[]{:S(2)}) %collective-permute-start.62) | collective-permute-done | bytes 65568 | tf_op jit(solution)/shard_map/ppermute | solution.py:20
  940.1 11.7 %collective-permute-done.65 = bf16[2,32,1024]{2,1,0:T(8,128)(2,1)S(1)} collective-permute-done((bf16[2,32,1024]{2,1,0:T(8,128)(2,1)S(1)}, bf16[2,32,1024]{2,1,0:T(8,128)(2,1)S(1)}, u32[]{:S(2)}, u32[]{:S(2)}) %collective-permute-start.65) | collective-permute-done | bytes 131104 | tf_op jit(solution)/shard_map/ppermute | solution.py:20
  952.8 9.8 all_gather.66
  964.1 8.6 all_gather.67
  986.3 13.1 %all_gather.64 = bf16[128,3072]{1,0:T(8,128)(2,1)S(1)} all-gather(bf16[32,3072]{1,0:T(8,128)(2,1)S(1)} %reshape.2380), channel_id=1, replica_groups=mesh['rep'=4,'grp'=8] {'rep'}, dimensions={0}, use_global_device_ids=true | all-gather | bytes 983040 | tf_op jit(solution)/shard_map/all_gather | solution.py:217
  999.4 12.1 %all_gather.65 = bf16[128,3072]{1,0:T(8,128)(2,1)S(1)} all-gather(bf16[32,3072]{1,0:T(8,128)(2,1)S(1)} %reshape.2383), channel_id=1, replica_groups=mesh['rep'=4,'grp'=8] {'rep'}, dimensions={0}, use_global_device_ids=true | all-gather | bytes 983040 | tf_op jit(solution)/shard_map/all_gather | solution.py:217
  1013.3 3.8 maximum_convert_fusion.1
  1017.2 4.0 all-gather.31.cloned.1.call-done
  1021.1 3.8 maximum_convert_fusion
  (427 shorter events, 184.0 us)
Async XLA Ops:
  7.2 32.1 %all-gather.13.cloned.1.call-start = ((), (), s32[]{:S(2)}) async-start(), calls=%async_computation | async-start | bytes 1769472 | tf_op jit(solution)/shard_map/all_gather | solution.py:191
  11.4 90.1 %all-gather.17.cloned.1.call-start = ((), (), s32[]{:S(2)}) async-start(), calls=%async_computation.2 | async-start | bytes 2359296 | tf_op jit(solution)/shard_map/all_gather | solution.py:191
  13.3 100.6 %all-gather.15.cloned.1.call-start = ((), (), s32[]{:S(2)}) async-start(), calls=%async_computation.1 | async-start | bytes 1966080 | tf_op jit(solution)/shard_map/all_gather | solution.py:195
  46.1 113.5 %all-gather.21.cloned.1.call-start = ((), (), s32[]{:S(2)}) async-start(), calls=%async_computation.4 | async-start | bytes 1769472 | tf_op jit(solution)/shard_map/all_gather | solution.py:191
  47.4 27.5 %collective-permute-start = (bf16[128,1024]{1,0:T(8,128)(2,1)S(1)}, bf16[128,1024]{1,0:T(8,128)(2,1)S(1)}, u32[]{:S(2)}, u32[]{:S(2)}) collective-permute-start(bf16[128,1024]{1,0:T(8,128)(2,1)S(1)} %get-tuple-element.106), channel_id=1, source_target_pairs={{0,4},{1,5},{2,6},{3,7},{4,0},{5,1},{6,2},{7,3},{8,12},{9,13},{10,... | collective-permute-start | bytes 786440 | tf_op jit(solution)/shard_map/ppermute | solution.py:20
  75.3 20.9 %collective-permute-start.2 = (bf16[2,128,1024]{2,1,0:T(8,128)(2,1)S(1)}, bf16[2,128,1024]{2,1,0:T(8,128)(2,1)S(1)}, u32[]{:S(2)}, u32[]{:S(2)}) collective-permute-start(bf16[2,128,1024]{2,1,0:T(8,128)(2,1)S(1)} %fusion.23), channel_id=1, source_target_pairs={{0,2},{1,3},{2,0},{3,1},{4,6},{5,7},{6,4},{7,5},{8,10},{9,11},{10,... | collective-permute-start | bytes 1572872 | tf_op jit(solution)/shard_map/ppermute | solution.py:20
  78.6 113.0 %all-gather.19.cloned.1.call-start = ((), (), s32[]{:S(2)}) async-start(), calls=%async_computation.3 | async-start | bytes 2621440 | tf_op jit(solution)/shard_map/all_gather | solution.py:195
  78.6 20.3 %collective-permute-start.1 = (bf16[2,128,1024]{2,1,0:T(8,128)(2,1)S(1)}, bf16[2,128,1024]{2,1,0:T(8,128)(2,1)S(1)}, u32[]{:S(2)}, u32[]{:S(2)}) collective-permute-start(bf16[2,128,1024]{2,1,0:T(8,128)(2,1)S(1)} %fusion.23), channel_id=1, source_target_pairs={{0,1},{1,0},{2,3},{3,2},{4,5},{5,4},{6,7},{7,6},{8,9},{9,8},{10,11... | collective-permute-start | bytes 1572872 | tf_op jit(solution)/shard_map/ppermute | solution.py:20
  79.5 43.0 %collective-permute-start.4 = (bf16[128,1024]{1,0:T(8,128)(2,1)S(1)}, bf16[128,1024]{1,0:T(8,128)(2,1)S(1)}, u32[]{:S(2)}, u32[]{:S(2)}) collective-permute-start(bf16[128,1024]{1,0:T(8,128)(2,1)S(1)} %get-tuple-element.104), channel_id=1, source_target_pairs={{0,4},{1,5},{2,6},{3,7},{4,0},{5,1},{6,2},{7,3},{8,12},{9,13},{10,... | collective-permute-start | bytes 786440 | tf_op jit(solution)/shard_map/ppermute | solution.py:20
  126.6 5.9 collective-permute-start.6
  131.4 133.3 %all-gather.23.cloned.1.call-start = ((), (), s32[]{:S(2)}) async-start(), calls=%async_computation.5 | async-start | bytes 1966080 | tf_op jit(solution)/shard_map/all_gather | solution.py:195
  133.9 16.0 %collective-permute-start.7 = (bf16[2,128,1024]{2,1,0:T(8,128)(2,1)S(1)}, bf16[2,128,1024]{2,1,0:T(8,128)(2,1)S(1)}, u32[]{:S(2)}, u32[]{:S(2)}) collective-permute-start(bf16[2,128,1024]{2,1,0:T(8,128)(2,1)S(1)} %fusion.46), channel_id=1, source_target_pairs={{0,2},{1,3},{2,0},{3,1},{4,6},{5,7},{6,4},{7,5},{8,10},{9,11},{10,... | collective-permute-start | bytes 1572872 | tf_op jit(solution)/shard_map/ppermute | solution.py:20
  155.7 23.2 %collective-permute-start.9 = (bf16[2,128,1024]{2,1,0:T(8,128)(2,1)}, bf16[2,128,1024]{2,1,0:T(8,128)(2,1)}, u32[]{:S(2)}, u32[]{:S(2)}) collective-permute-start(bf16[2,128,1024]{2,1,0:T(8,128)(2,1)} %get-tuple-element.69), channel_id=1, source_target_pairs={{0,2},{1,3},{2,0},{3,1},{4,6},{5,7},{6,4},{7,5},{8,10},{9,11},{10,... | collective-permute-start | bytes 1572872 | tf_op jit(solution)/shard_map/ppermute | solution.py:20
  155.9 29.9 %collective-permute-start.8 = (bf16[2,128,1024]{2,1,0:T(8,128)(2,1)}, bf16[2,128,1024]{2,1,0:T(8,128)(2,1)}, u32[]{:S(2)}, u32[]{:S(2)}) collective-permute-start(bf16[2,128,1024]{2,1,0:T(8,128)(2,1)} %get-tuple-element.69), channel_id=1, source_target_pairs={{0,1},{1,0},{2,3},{3,2},{4,5},{5,4},{6,7},{7,6},{8,9},{9,8},{10,11... | collective-permute-start | bytes 1572872 | tf_op jit(solution)/shard_map/ppermute | solution.py:20
  157.4 49.3 %collective-permute-start.11 = (bf16[512,1024]{1,0:T(8,128)(2,1)}, bf16[512,1024]{1,0:T(8,128)(2,1)}, u32[]{:S(2)}, u32[]{:S(2)}) collective-permute-start(bf16[512,1024]{1,0:T(8,128)(2,1)} %get-tuple-element.93), channel_id=1, source_target_pairs={{0,4},{1,5},{2,6},{3,7},{4,0},{5,1},{6,2},{7,3},{8,12},{9,13},{10,... | collective-permute-start | bytes 3145736 | tf_op jit(solution)/shard_map/ppermute | solution.py:20
  178.9 10.7 %collective-permute-start.10 = (bf16[2,128,1024]{2,1,0:T(8,128)(2,1)}, bf16[2,128,1024]{2,1,0:T(8,128)(2,1)}, u32[]{:S(2)}, u32[]{:S(2)}) collective-permute-start(bf16[2,128,1024]{2,1,0:T(8,128)(2,1)} %collective-permute-done.9), channel_id=1, source_target_pairs={{0,1},{1,0},{2,3},{3,2},{4,5},{5,4},{6,7},{7,6},{8,9},{9,8},{10,11... | collective-permute-start | bytes 1572872 | tf_op jit(solution)/shard_map/ppermute | solution.py:20
  185.8 94.0 %all-gather.25.cloned.1.call-start = ((), (), s32[]{:S(2)}) async-start(), calls=%async_computation.6 | async-start | bytes 2359296 | tf_op jit(solution)/shard_map/all_gather | solution.py:191
  213.5 5.8 collective-permute-start.12
  217.1 17.8 %collective-permute-start.14 = (bf16[2,128,1024]{2,1,0:T(8,128)(2,1)}, bf16[2,128,1024]{2,1,0:T(8,128)(2,1)}, u32[]{:S(2)}, u32[]{:S(2)}) collective-permute-start(bf16[2,128,1024]{2,1,0:T(8,128)(2,1)} %fusion.44), channel_id=1, source_target_pairs={{0,2},{1,3},{2,0},{3,1},{4,6},{5,7},{6,4},{7,5},{8,10},{9,11},{10,... | collective-permute-start | bytes 1572872 | tf_op jit(solution)/shard_map/ppermute | solution.py:20
  219.1 112.2 %all-gather.27.cloned.1.call-start = ((), (), s32[]{:S(2)}) async-start(), calls=%async_computation.7 | async-start | bytes 2621440 | tf_op jit(solution)/shard_map/all_gather | solution.py:195
  240.3 19.0 %collective-permute-start.16 = (bf16[2,128,1024]{2,1,0:T(8,128)(2,1)S(1)}, bf16[2,128,1024]{2,1,0:T(8,128)(2,1)S(1)}, u32[]{:S(2)}, u32[]{:S(2)}) collective-permute-start(bf16[2,128,1024]{2,1,0:T(8,128)(2,1)S(1)} %get-tuple-element.63), channel_id=1, source_target_pairs={{0,2},{1,3},{2,0},{3,1},{4,6},{5,7},{6,4},{7,5},{8,10},{9,11},{10,... | collective-permute-start | bytes 1572872 | tf_op jit(solution)/shard_map/ppermute | solution.py:20
  240.3 21.8 %collective-permute-start.15 = (bf16[2,128,1024]{2,1,0:T(8,128)(2,1)S(1)}, bf16[2,128,1024]{2,1,0:T(8,128)(2,1)S(1)}, u32[]{:S(2)}, u32[]{:S(2)}) collective-permute-start(bf16[2,128,1024]{2,1,0:T(8,128)(2,1)S(1)} %get-tuple-element.63), channel_id=1, source_target_pairs={{0,1},{1,0},{2,3},{3,2},{4,5},{5,4},{6,7},{7,6},{8,9},{9,8},{10,11... | collective-permute-start | bytes 1572872 | tf_op jit(solution)/shard_map/ppermute | solution.py:20
  259.4 15.5 %collective-permute-start.18 = (bf16[128,1024]{1,0:T(8,128)(2,1)S(1)}, bf16[128,1024]{1,0:T(8,128)(2,1)}, u32[]{:S(2)}, u32[]{:S(2)}) collective-permute-start(bf16[128,1024]{1,0:T(8,128)(2,1)S(1)} %copy-done.34), channel_id=1, source_target_pairs={{0,4},{1,5},{2,6},{3,7},{4,0},{5,1},{6,2},{7,3},{8,12},{9,13},{10,... | collective-permute-start | bytes 786440 | tf_op jit(solution)/shard_map/ppermute | solution.py:20
  279.8 13.7 %collective-permute-start.20 = (bf16[2,128,1024]{2,1,0:T(8,128)(2,1)}, bf16[2,128,1024]{2,1,0:T(8,128)(2,1)}, u32[]{:S(2)}, u32[]{:S(2)}) collective-permute-start(bf16[2,128,1024]{2,1,0:T(8,128)(2,1)} %get-tuple-element.85), channel_id=1, source_target_pairs={{0,1},{1,0},{2,3},{3,2},{4,5},{5,4},{6,7},{7,6},{8,9},{9,8},{10,11... | collective-permute-start | bytes 1572872 | tf_op jit(solution)/shard_map/ppermute | solution.py:20
  292.5 535.9 %all-reduce.11.cloned.1.call-start = ((), (), s32[]{:S(2)}) async-start(), calls=%async_computation.12 | async-start | bytes 25165824
  295.1 13.9 %collective-permute-start.21 = (bf16[2,128,1024]{2,1,0:T(8,128)(2,1)S(1)}, bf16[2,128,1024]{2,1,0:T(8,128)(2,1)S(1)}, u32[]{:S(2)}, u32[]{:S(2)}) collective-permute-start(bf16[2,128,1024]{2,1,0:T(8,128)(2,1)S(1)} %fusion.42), channel_id=1, source_target_pairs={{0,2},{1,3},{2,0},{3,1},{4,6},{5,7},{6,4},{7,5},{8,10},{9,11},{10,... | collective-permute-start | bytes 1572872 | tf_op jit(solution)/shard_map/ppermute | solution.py:20
  313.6 13.1 %collective-permute-start.23 = (bf16[2,128,1024]{2,1,0:T(8,128)(2,1)S(1)}, bf16[2,128,1024]{2,1,0:T(8,128)(2,1)S(1)}, u32[]{:S(2)}, u32[]{:S(2)}) collective-permute-start(bf16[2,128,1024]{2,1,0:T(8,128)(2,1)S(1)} %get-tuple-element.57), channel_id=1, source_target_pairs={{0,2},{1,3},{2,0},{3,1},{4,6},{5,7},{6,4},{7,5},{8,10},{9,11},{10,... | collective-permute-start | bytes 1572872 | tf_op jit(solution)/shard_map/ppermute | solution.py:20
  313.8 14.9 %collective-permute-start.22 = (bf16[2,128,1024]{2,1,0:T(8,128)(2,1)S(1)}, bf16[2,128,1024]{2,1,0:T(8,128)(2,1)S(1)}, u32[]{:S(2)}, u32[]{:S(2)}) collective-permute-start(bf16[2,128,1024]{2,1,0:T(8,128)(2,1)S(1)} %get-tuple-element.57), channel_id=1, source_target_pairs={{0,1},{1,0},{2,3},{3,2},{4,5},{5,4},{6,7},{7,6},{8,9},{9,8},{10,11... | collective-permute-start | bytes 1572872 | tf_op jit(solution)/shard_map/ppermute | solution.py:20
  326.7 49.3 %collective-permute-start.25 = (bf16[512,1024]{1,0:T(8,128)(2,1)}, bf16[512,1024]{1,0:T(8,128)(2,1)}, u32[]{:S(2)}, u32[]{:S(2)}) collective-permute-start(bf16[512,1024]{1,0:T(8,128)(2,1)} %get-tuple-element.92), channel_id=1, source_target_pairs={{0,4},{1,5},{2,6},{3,7},{4,0},{5,1},{6,2},{7,3},{8,12},{9,13},{10,... | collective-permute-start | bytes 3145736 | tf_op jit(solution)/shard_map/ppermute | solution.py:20
  381.9 5.7 collective-permute-start.26
  383.9 19.6 %collective-permute-start.28 = (bf16[2,128,1024]{2,1,0:T(8,128)(2,1)S(1)}, bf16[2,128,1024]{2,1,0:T(8,128)(2,1)S(1)}, u32[]{:S(2)}, u32[]{:S(2)}) collective-permute-start(bf16[2,128,1024]{2,1,0:T(8,128)(2,1)S(1)} %fusion.40), channel_id=1, source_target_pairs={{0,2},{1,3},{2,0},{3,1},{4,6},{5,7},{6,4},{7,5},{8,10},{9,11},{10,... | collective-permute-start | bytes 1572872 | tf_op jit(solution)/shard_map/ppermute | solution.py:20
  384.1 19.7 %collective-permute-start.30 = (bf16[128,1024]{1,0:T(8,128)(2,1)S(1)}, bf16[128,1024]{1,0:T(8,128)(2,1)S(1)}, u32[]{:S(2)}, u32[]{:S(2)}) collective-permute-start(bf16[128,1024]{1,0:T(8,128)(2,1)S(1)} %get-tuple-element.99), channel_id=1, source_target_pairs={{0,4},{1,5},{2,6},{3,7},{4,0},{5,1},{6,2},{7,3},{8,12},{9,13},{10,... | collective-permute-start | bytes 786440 | tf_op jit(solution)/shard_map/ppermute | solution.py:20
  405.7 13.2 %collective-permute-start.32 = (bf16[2,128,1024]{2,1,0:T(8,128)(2,1)S(1)}, bf16[2,128,1024]{2,1,0:T(8,128)(2,1)S(1)}, u32[]{:S(2)}, u32[]{:S(2)}) collective-permute-start(bf16[2,128,1024]{2,1,0:T(8,128)(2,1)S(1)} %get-tuple-element.53), channel_id=1, source_target_pairs={{0,2},{1,3},{2,0},{3,1},{4,6},{5,7},{6,4},{7,5},{8,10},{9,11},{10,... | collective-permute-start | bytes 1572872 | tf_op jit(solution)/shard_map/ppermute | solution.py:20
  407.2 11.7 %collective-permute-start.31 = (bf16[2,128,1024]{2,1,0:T(8,128)(2,1)S(1)}, bf16[2,128,1024]{2,1,0:T(8,128)(2,1)S(1)}, u32[]{:S(2)}, u32[]{:S(2)}) collective-permute-start(bf16[2,128,1024]{2,1,0:T(8,128)(2,1)S(1)} %get-tuple-element.53), channel_id=1, source_target_pairs={{0,1},{1,0},{2,3},{3,2},{4,5},{5,4},{6,7},{7,6},{8,9},{9,8},{10,11... | collective-permute-start | bytes 1572872 | tf_op jit(solution)/shard_map/ppermute | solution.py:20
  432.7 14.0 %collective-permute-start.36 = (bf16[2,128,1024]{2,1,0:T(8,128)(2,1)S(1)}, bf16[2,128,1024]{2,1,0:T(8,128)(2,1)S(1)}, u32[]{:S(2)}, u32[]{:S(2)}) collective-permute-start(bf16[2,128,1024]{2,1,0:T(8,128)(2,1)S(1)} %fusion.38), channel_id=1, source_target_pairs={{0,2},{1,3},{2,0},{3,1},{4,6},{5,7},{6,4},{7,5},{8,10},{9,11},{10,... | collective-permute-start | bytes 1572872 | tf_op jit(solution)/shard_map/ppermute | solution.py:20
  448.5 13.2 %collective-permute-start.38 = (bf16[2,128,1024]{2,1,0:T(8,128)(2,1)S(1)}, bf16[2,128,1024]{2,1,0:T(8,128)(2,1)S(1)}, u32[]{:S(2)}, u32[]{:S(2)}) collective-permute-start(bf16[2,128,1024]{2,1,0:T(8,128)(2,1)S(1)} %get-tuple-element.49), channel_id=1, source_target_pairs={{0,2},{1,3},{2,0},{3,1},{4,6},{5,7},{6,4},{7,5},{8,10},{9,11},{10,... | collective-permute-start | bytes 1572872 | tf_op jit(solution)/shard_map/ppermute | solution.py:20
  450.3 11.4 %collective-permute-start.37 = (bf16[2,128,1024]{2,1,0:T(8,128)(2,1)S(1)}, bf16[2,128,1024]{2,1,0:T(8,128)(2,1)S(1)}, u32[]{:S(2)}, u32[]{:S(2)}) collective-permute-start(bf16[2,128,1024]{2,1,0:T(8,128)(2,1)S(1)} %get-tuple-element.49), channel_id=1, source_target_pairs={{0,1},{1,0},{2,3},{3,2},{4,5},{5,4},{6,7},{7,6},{8,9},{9,8},{10,11... | collective-permute-start | bytes 1572872 | tf_op jit(solution)/shard_map/ppermute | solution.py:20
  480.5 14.0 %collective-permute-start.42 = (bf16[2,128,1024]{2,1,0:T(8,128)(2,1)S(1)}, bf16[2,128,1024]{2,1,0:T(8,128)(2,1)S(1)}, u32[]{:S(2)}, u32[]{:S(2)}) collective-permute-start(bf16[2,128,1024]{2,1,0:T(8,128)(2,1)S(1)} %fusion.36), channel_id=1, source_target_pairs={{0,2},{1,3},{2,0},{3,1},{4,6},{5,7},{6,4},{7,5},{8,10},{9,11},{10,... | collective-permute-start | bytes 1572872 | tf_op jit(solution)/shard_map/ppermute | solution.py:20
  496.2 13.2 %collective-permute-start.44 = (bf16[2,128,1024]{2,1,0:T(8,128)(2,1)S(1)}, bf16[2,128,1024]{2,1,0:T(8,128)(2,1)S(1)}, u32[]{:S(2)}, u32[]{:S(2)}) collective-permute-start(bf16[2,128,1024]{2,1,0:T(8,128)(2,1)S(1)} %get-tuple-element.45), channel_id=1, source_target_pairs={{0,2},{1,3},{2,0},{3,1},{4,6},{5,7},{6,4},{7,5},{8,10},{9,11},{10,... | collective-permute-start | bytes 1572872 | tf_op jit(solution)/shard_map/ppermute | solution.py:20
  498.0 15.5 %collective-permute-start.43 = (bf16[2,128,1024]{2,1,0:T(8,128)(2,1)S(1)}, bf16[2,128,1024]{2,1,0:T(8,128)(2,1)S(1)}, u32[]{:S(2)}, u32[]{:S(2)}) collective-permute-start(bf16[2,128,1024]{2,1,0:T(8,128)(2,1)S(1)} %get-tuple-element.45), channel_id=1, source_target_pairs={{0,1},{1,0},{2,3},{3,2},{4,5},{5,4},{6,7},{7,6},{8,9},{9,8},{10,11... | collective-permute-start | bytes 1572872 | tf_op jit(solution)/shard_map/ppermute | solution.py:20
  523.6 5.9 collective-permute-start.47
  529.4 8.2 collective-permute-start.46
  529.6 14.4 %collective-permute-start.48 = (bf16[2,128,1024]{2,1,0:T(8,128)(2,1)S(1)}, bf16[2,128,1024]{2,1,0:T(8,128)(2,1)S(1)}, u32[]{:S(2)}, u32[]{:S(2)}) collective-permute-start(bf16[2,128,1024]{2,1,0:T(8,128)(2,1)S(1)} %fusion.34), channel_id=1, source_target_pairs={{0,2},{1,3},{2,0},{3,1},{4,6},{5,7},{6,4},{7,5},{8,10},{9,11},{10,... | collective-permute-start | bytes 1572872 | tf_op jit(solution)/shard_map/ppermute | solution.py:20
  546.1 13.5 %collective-permute-start.50 = (bf16[2,128,1024]{2,1,0:T(8,128)(2,1)S(1)}, bf16[2,128,1024]{2,1,0:T(8,128)(2,1)S(1)}, u32[]{:S(2)}, u32[]{:S(2)}) collective-permute-start(bf16[2,128,1024]{2,1,0:T(8,128)(2,1)S(1)} %get-tuple-element.41), channel_id=1, source_target_pairs={{0,2},{1,3},{2,0},{3,1},{4,6},{5,7},{6,4},{7,5},{8,10},{9,11},{10,... | collective-permute-start | bytes 1572872 | tf_op jit(solution)/shard_map/ppermute | solution.py:20
  552.2 12.8 %collective-permute-start.49 = (bf16[2,128,1024]{2,1,0:T(8,128)(2,1)S(1)}, bf16[2,128,1024]{2,1,0:T(8,128)(2,1)S(1)}, u32[]{:S(2)}, u32[]{:S(2)}) collective-permute-start(bf16[2,128,1024]{2,1,0:T(8,128)(2,1)S(1)} %get-tuple-element.41), channel_id=1, source_target_pairs={{0,1},{1,0},{2,3},{3,2},{4,5},{5,4},{6,7},{7,6},{8,9},{9,8},{10,11... | collective-permute-start | bytes 1572872 | tf_op jit(solution)/shard_map/ppermute | solution.py:20
  583.2 430.2 %all-gather.33.cloned.1.call-start = ((), (), s32[]{:S(2)}) async-start(), calls=%async_computation.10 | async-start | bytes 1310720 | tf_op jit(solution)/shard_map/all_gather | solution.py:234
  587.2 244.7 %collective-permute-start.52 = (bf16[2,128,1024]{2,1,0:T(8,128)(2,1)S(1)}, bf16[2,128,1024]{2,1,0:T(8,128)(2,1)S(1)}, u32[]{:S(2)}, u32[]{:S(2)}) collective-permute-start(bf16[2,128,1024]{2,1,0:T(8,128)(2,1)S(1)} %get-tuple-element.74), channel_id=1, source_target_pairs={{0,1},{1,0},{2,3},{3,2},{4,5},{5,4},{6,7},{7,6},{8,9},{9,8},{10,11... | collective-permute-start | bytes 1572872 | tf_op jit(solution)/shard_map/ppermute | solution.py:20
  588.9 243.0 %collective-permute-start.54 = (bf16[2,128,1024]{2,1,0:T(8,128)(2,1)S(1)}, bf16[2,128,1024]{2,1,0:T(8,128)(2,1)}, u32[]{:S(2)}, u32[]{:S(2)}) collective-permute-start(bf16[2,128,1024]{2,1,0:T(8,128)(2,1)S(1)} %fusion.32), channel_id=1, source_target_pairs={{0,2},{1,3},{2,0},{3,1},{4,6},{5,7},{6,4},{7,5},{8,10},{9,11},{10,... | collective-permute-start | bytes 1572872 | tf_op jit(solution)/shard_map/ppermute | solution.py:20
  590.7 17.3 %collective-permute-start.29 = (bf16[128,1024]{1,0:T(8,128)(2,1)S(1)}, bf16[128,1024]{1,0:T(8,128)(2,1)S(1)}, u32[]{:S(2)}, u32[]{:S(2)}) collective-permute-start(bf16[128,1024]{1,0:T(8,128)(2,1)S(1)} %get-tuple-element.102), channel_id=1, source_target_pairs={{0,4},{1,5},{2,6},{3,7},{4,0},{5,1},{6,2},{7,3},{8,12},{9,13},{10,... | collective-permute-start | bytes 786440 | tf_op jit(solution)/shard_map/ppermute | solution.py:20
  829.4 14.7 %collective-permute-start.70 = (bf16[128,1024]{1,0:T(8,128)(2,1)S(1)}, bf16[128,1024]{1,0:T(8,128)(2,1)S(1)}, u32[]{:S(2)}, u32[]{:S(2)}) collective-permute-start(bf16[128,1024]{1,0:T(8,128)(2,1)S(1)} %dynamic-slice_bitcast_fusion.2), channel_id=1, source_target_pairs={{0,4},{1,5},{2,6},{3,7},{4,0},{5,1},{6,2},{7,3},{8,12},{9,13},{10,... | collective-permute-start | bytes 786440 | tf_op jit(solution)/shard_map/ppermute | solution.py:20
  845.8 167.5 %all-gather.35.cloned.1.call-start = ((), (), s32[]{:S(2)}) async-start(), calls=%async_computation.11 | async-start | bytes 1310720 | tf_op jit(solution)/shard_map/all_gather | solution.py:234
  846.3 42.5 %collective-permute-start.55 = (bf16[128,1024]{1,0:T(8,128)(2,1)S(1)}, bf16[128,1024]{1,0:T(8,128)(2,1)S(1)}, u32[]{:S(2)}, u32[]{:S(2)}) collective-permute-start(bf16[128,1024]{1,0:T(8,128)(2,1)S(1)} %get-tuple-element.98), channel_id=1, source_target_pairs={{0,4},{1,5},{2,6},{3,7},{4,0},{5,1},{6,2},{7,3},{8,12},{9,13},{10,... | collective-permute-start | bytes 786440 | tf_op jit(solution)/shard_map/ppermute | solution.py:20
  890.8 27.4 %collective-permute-start.71 = (bf16[128,1024]{1,0:T(8,128)(2,1)S(1)}, bf16[128,1024]{1,0:T(8,128)(2,1)S(1)}, u32[]{:S(2)}, u32[]{:S(2)}) collective-permute-start(bf16[128,1024]{1,0:T(8,128)(2,1)S(1)} %dynamic-slice_bitcast_fusion), channel_id=1, source_target_pairs={{0,4},{1,5},{2,6},{3,7},{4,0},{5,1},{6,2},{7,3},{8,12},{9,13},{10,... | collective-permute-start | bytes 786440 | tf_op jit(solution)/shard_map/ppermute | solution.py:20
  892.8 31.0 %collective-permute-start.64 = (bf16[4,32,1024]{2,1,0:T(8,128)(2,1)S(1)}, bf16[4,32,1024]{2,1,0:T(8,128)(2,1)S(1)}, u32[]{:S(2)}, u32[]{:S(2)}) collective-permute-start(bf16[4,32,1024]{2,1,0:T(8,128)(2,1)S(1)} %dynamic-slice_bitcast_fusion.5), channel_id=1, source_target_pairs={{0,4},{1,5},{2,6},{3,7},{4,0},{5,1},{6,2},{7,3},{8,12},{9,13},{10,... | collective-permute-start | bytes 786440 | tf_op jit(solution)/shard_map/ppermute | solution.py:20
  895.7 78.0 %collective-permute-start.67 = (bf16[4,32,1024]{2,1,0:T(8,128)(2,1)S(1)}, bf16[4,32,1024]{2,1,0:T(8,128)(2,1)S(1)}, u32[]{:S(2)}, u32[]{:S(2)}) collective-permute-start(bf16[4,32,1024]{2,1,0:T(8,128)(2,1)S(1)} %dynamic-slice_bitcast_fusion.4), channel_id=1, source_target_pairs={{0,4},{1,5},{2,6},{3,7},{4,0},{5,1},{6,2},{7,3},{8,12},{9,13},{10,... | collective-permute-start | bytes 786440 | tf_op jit(solution)/shard_map/ppermute | solution.py:20
  897.3 41.9 %collective-permute-start.62 = (bf16[32,1024]{1,0:T(8,128)(2,1)}, bf16[32,1024]{1,0:T(8,128)(2,1)S(1)}, u32[]{:S(2)}, u32[]{:S(2)}) collective-permute-start(bf16[32,1024]{1,0:T(8,128)(2,1)} %dynamic-slice_bitcast_fusion.25), channel_id=1, source_target_pairs={{0,4},{1,5},{2,6},{3,7},{4,0},{5,1},{6,2},{7,3},{8,12},{9,13},{10,... | collective-permute-start | bytes 196616 | tf_op jit(solution)/shard_map/ppermute | solution.py:20
  901.7 50.2 %collective-permute-start.63 = (bf16[32,1024]{1,0:T(8,128)(2,1)}, bf16[32,1024]{1,0:T(8,128)(2,1)}, u32[]{:S(2)}, u32[]{:S(2)}) collective-permute-start(bf16[32,1024]{1,0:T(8,128)(2,1)} %dynamic-slice_bitcast_fusion.23), channel_id=1, source_target_pairs={{0,4},{1,5},{2,6},{3,7},{4,0},{5,1},{6,2},{7,3},{8,12},{9,13},{10,... | collective-permute-start | bytes 196616 | tf_op jit(solution)/shard_map/ppermute | solution.py:20
  919.9 97.3 %all-gather.29.cloned.1.call-start = ((), (), s32[]{:S(2)}) async-start(), calls=%async_computation.8 | async-start | bytes 1310720 | tf_op jit(solution)/shard_map/all_gather | solution.py:217
  921.7 52.2 %collective-permute-start.56 = (bf16[4,32,768]{2,1,0:T(8,128)(2,1)S(1)}, bf16[4,32,768]{2,1,0:T(8,128)(2,1)}, u32[]{:S(2)}, u32[]{:S(2)}) collective-permute-start(bf16[4,32,768]{2,1,0:T(8,128)(2,1)S(1)} %dynamic-slice_bitcast_fusion.14), channel_id=1, source_target_pairs={{0,4},{1,5},{2,6},{3,7},{4,0},{5,1},{6,2},{7,3},{8,12},{9,13},{10,... | collective-permute-start | bytes 589832 | tf_op jit(solution)/shard_map/ppermute | solution.py:20
  923.8 55.2 %collective-permute-start.59 = (bf16[4,32,768]{2,1,0:T(8,128)(2,1)S(1)}, bf16[4,32,768]{2,1,0:T(8,128)(2,1)S(1)}, u32[]{:S(2)}, u32[]{:S(2)}) collective-permute-start(bf16[4,32,768]{2,1,0:T(8,128)(2,1)S(1)} %dynamic-slice_bitcast_fusion.13), channel_id=1, source_target_pairs={{0,4},{1,5},{2,6},{3,7},{4,0},{5,1},{6,2},{7,3},{8,12},{9,13},{10,... | collective-permute-start | bytes 589832 | tf_op jit(solution)/shard_map/ppermute | solution.py:20
  939.2 12.5 %collective-permute-start.65 = (bf16[2,32,1024]{2,1,0:T(8,128)(2,1)S(1)}, bf16[2,32,1024]{2,1,0:T(8,128)(2,1)S(1)}, u32[]{:S(2)}, u32[]{:S(2)}) collective-permute-start(bf16[2,32,1024]{2,1,0:T(8,128)(2,1)S(1)} %get-tuple-element.110), channel_id=1, source_target_pairs={{0,2},{1,3},{2,0},{3,1},{4,6},{5,7},{6,4},{7,5},{8,10},{9,11},{10,... | collective-permute-start | bytes 393224 | tf_op jit(solution)/shard_map/ppermute | solution.py:20
  951.8 10.8 %collective-permute-start.66 = (bf16[2,32,1024]{2,1,0:T(8,128)(2,1)S(1)}, bf16[2,32,1024]{2,1,0:T(8,128)(2,1)S(1)}, u32[]{:S(2)}, u32[]{:S(2)}) collective-permute-start(bf16[2,32,1024]{2,1,0:T(8,128)(2,1)S(1)} %get-tuple-element.108), channel_id=1, source_target_pairs={{0,1},{1,0},{2,3},{3,2},{4,5},{5,4},{6,7},{7,6},{8,9},{9,8},{10,11... | collective-permute-start | bytes 393224 | tf_op jit(solution)/shard_map/ppermute | solution.py:20
  964.0 57.1 %all-gather.31.cloned.1.call-start = ((), (), s32[]{:S(2)}) async-start(), calls=%async_computation.9 | async-start | bytes 1310720 | tf_op jit(solution)/shard_map/all_gather | solution.py:217
  974.9 6.7 collective-permute-start.57
  (72 other events, 1651.2 us)
Sparse Core Ops, SparseCore 0:
  11.5 27.7 all-gather.12
  41.4 39.4 all-gather.16
  83.4 30.4 all-gather.14
  115.4 26.0 all-gather.20
  143.7 35.9 all-gather.18
  185.9 29.2 all-gather.22
  219.2 34.8 all-gather.24
  292.7 35.7 all-gather.26
  583.3 245.1 all-reduce.10
  846.0 26.7 all-gather.32
  920.0 25.9 all-gather.34
  964.1 25.1 all-gather.28
  991.7 29.3 all-gather.30

commit v2 on v1

--- a/solution.py
+++ b/solution.py
@@ -1,4 +1,5 @@
 import functools
+import types
 
 import jax
 import jax.numpy as jnp
@@ -157,28 +158,637 @@
     )(qkv, lse, grad)
 
 
-def gather4(mine, place):
-    other = core(mine)
-    across = near(mine)
-    corner = core(across)
-    halves, rows, width = mine.shape
-    whole = jnp.zeros((halves, 4, rows, width), mine.dtype)
-    for value, where in ((mine, place), (other, place ^ 1), (across, place ^ 2), (corner, place ^ 3)):
-        whole = lax.dynamic_update_slice(whole, value[:, None], (0, where, 0, 0))
-    return whole.reshape(halves * 4 * rows, width)
-
-
-def scatter4(part, place):
-    total, width = part.shape
-    part = part.reshape(2, 4, total // 8, width)
-
-    def term(where):
-        return lax.dynamic_slice(part, (0, where, 0, 0), (2, 1, total // 8, width))[:, 0]
-
-    across = core(term(place ^ 3).astype(BF)).astype(F32) + term(place ^ 2)
-    across = near(across.astype(BF))
-    mine = core(term(place ^ 1).astype(BF)).astype(F32) + term(place)
-    return (mine + across.astype(F32)).reshape(total // 4, width)
+MESH_ID = pl.DeviceIdType.MESH
+TOK = 128
+
+
+class Place:
+    def __init__(self):
+        rep, grp = lax.axis_index("rep"), lax.axis_index("grp")
+        self.rep, self.grp = rep, grp
+        self.x, self.y = lax.rem(rep, 2), lax.div(rep, 2)
+        self.t, self.upper = lax.rem(grp, 4), lax.div(grp, 4)
+        self.c, self.side = lax.rem(grp, 2), lax.div(self.t, 2)
+        base = self.upper * 4
+        self.core = (rep, base + self.side * 2 + 1 - self.c)
+        self.near = (rep, base + (1 - self.side) * 2 + self.c)
+        self.far = (rep, (1 - self.upper) * 4 + self.t)
+        self.along_x = (self.y * 2 + 1 - self.x, grp)
+        self.along_y = ((1 - self.y) * 2 + self.x, grp)
+        self.near_t = (1 - self.side) * 2 + self.c
+
+
+class Copies:
+    def __init__(self, send, recv, here):
+        self.sems, self.here = (send, recv), here
+        self.sent, self.local_count, self.stores = [], 0, []
+
+    def remote(self, source, target, device):
+        at = len(self.sent)
+        copy = pltpu.make_async_remote_copy(
+            src_ref=source,
+            dst_ref=target,
+            send_sem=self.sems[0].at[at],
+            recv_sem=self.sems[1].at[at],
+            device_id=device,
+            device_id_type=MESH_ID,
+        )
+        copy.start()
+        self.sent.append(copy)
+        return copy
+
+    def local(self, source, target):
+        copy = pltpu.make_async_copy(source, target, self.here.at[self.local_count])
+        self.local_count += 1
+        copy.start()
+        return copy
+
+    def store(self, source, target):
+        self.stores.append(self.local(source, target))
+
+    def finish(self):
+        for copy in self.sent:
+            copy.wait_send()
+        for copy in self.stores:
+            copy.wait()
+
+
+def meet(devices):
+    barrier = pltpu.get_barrier_semaphore()
+    for device in devices:
+        pl.semaphore_signal(barrier, inc=1, device_id=device, device_id_type=MESH_ID)
+    pl.semaphore_wait(barrier, len(devices))
+
+
+def loop(count, step):
+    def run(index, carry):
+        step(index)
+        return carry
+
+    lax.fori_loop(0, count, run, 0)
+
+
+def tile_of(index, size):
+    return pl.ds(pl.multiple_of(index * size, size), size)
+
+
+def times(left, right_ref, tile, sink):
+    def step(index):
+        at = tile_of(index, tile)
+        sink(at, dot(left(), right_ref[:, at]))
+
+    loop(right_ref.shape[1] // tile, step)
+
+
+def times_rows(left, right_ref, tile, sink):
+    def step(index):
+        at = tile_of(index, tile)
+        sink(at, dot_nt(left(), right_ref[at, :]))
+
+    loop(right_ref.shape[0] // tile, step)
+
+
+def gram(left_ref, right_ref, tile, out_ref):
+    def step(index):
+        at = tile_of(index, tile)
+        out_ref[at, :] = dot_tn(left_ref[:, at], right_ref[...]).astype(BF)
+
+    loop(left_ref.shape[1] // tile, step)
+
+
+class Gather:
+    def __init__(self, copies, place, buf):
+        self.copies, self.place, self.buf = copies, place, buf
+        self.flight = {}
+
+    def rows(self, stream, where):
+        start = (stream * 4 + where) * TOK
+        return pl.ds(pl.multiple_of(start, TOK), TOK)
+
+    def pair(self, stream, side):
+        start = (stream * 4 + side * 2) * TOK
+        return pl.ds(pl.multiple_of(start, TOK), 2 * TOK)
+
+    def start(self, stream, block):
+        at = self.rows(stream, self.place.t)
+        self.buf[at, :] = block
+        mine = self.buf.at[at, :]
+        across = self.copies.remote(mine, mine, self.place.near)
+        beside = self.copies.remote(mine, mine, self.place.core)
+        self.flight[stream] = [across, beside]
+
+    def wait_chip(self, stream):
+        self.flight[stream][1].wait_recv()
+
+    def forward(self, stream):
+        self.flight[stream][0].wait_recv()
+        got = self.buf.at[self.rows(stream, self.place.near_t), :]
+        self.flight[stream].append(self.copies.remote(got, got, self.place.core))
+
+    def wait_rest(self, stream):
+        self.flight[stream][2].wait_recv()
+
+
+class Scatter:
+    def __init__(self, copies, place, ns, name):
+        self.copies, self.place = copies, place
+        self.away, self.own, self.give, self.take, self.send, self.got = (
+            getattr(ns, name + part) for part in ("away", "own", "give", "take", "send", "got")
+        )
+        self.flight = {}
+
+    def push(self, stream, product):
+        place, copies = self.place, self.copies
+        mine = pl.ds(pl.multiple_of(place.c * TOK, TOK), TOK)
+        other = pl.ds(pl.multiple_of((1 - place.c) * TOK, TOK), TOK)
+
+        def to_away(at, value):
+            self.away[:, at] = value
+
+        def to_own(at, value):
+            self.own[stream, :, at] = value
+
+        product(1 - place.side, to_away)
+        self.give[stream, 0] = self.away[other, :].astype(BF)
+        first = copies.remote(self.give.at[stream, 0], self.take.at[stream, 0], place.core)
+        product(place.side, to_own)
+        first.wait_recv()
+        self.send[stream] = (self.away[mine, :] + self.take[stream, 0].astype(F32)).astype(BF)
+        across = copies.remote(self.send.at[stream], self.got.at[stream], place.near)
+        self.give[stream, 1] = self.own[stream, other, :].astype(BF)
+        second = copies.remote(self.give.at[stream, 1], self.take.at[stream, 1], place.core)
+        self.flight[stream] = (second, across)
+
+    def result(self, stream):
+        second, across = self.flight[stream]
+        mine = pl.ds(pl.multiple_of(self.place.c * TOK, TOK), TOK)
+        second.wait_recv()
+        total = self.own[stream, mine, :] + self.take[stream, 1].astype(F32)
+        across.wait_recv()
+        return total + self.got[stream].astype(F32)
+
+
+def scatter_scratch(name, width):
+    return {
+        name + "away": pltpu.VMEM((2 * TOK, width), F32),
+        name + "own": pltpu.VMEM((2, 2 * TOK, width), F32),
+        name + "give": pltpu.VMEM((2, 2, TOK, width), BF),
+        name + "take": pltpu.VMEM((2, 2, TOK, width), BF),
+        name + "send": pltpu.VMEM((2, TOK, width), BF),
+        name + "got": pltpu.VMEM((2, TOK, width), BF),
+    }
+
+
+def gelu_both(x):
+    cubic = x * x * 0.044715
+    bent = jnp.tanh(0.7978845608028654 * (x + cubic * x))
+    half = 0.5 * (1.0 + bent)
+    slope = half + 0.5 * x * (1.0 - bent * bent) * (0.7978845608028654 * (1.0 + 3.0 * cubic))
+    return x * half, slope
+
+
+def norm_back_in(values, gain, grad):
+    rstd = lax.rsqrt(jnp.mean(values * values, axis=-1, keepdims=True) + EPS)
+    hat = values * rstd
+    scaled = grad * gain
+    back = rstd * (scaled - hat * jnp.mean(scaled * hat, axis=-1, keepdims=True))
+    return back, jnp.sum(grad * hat, axis=0, keepdims=True)
+
+
+def launch(name, body, inputs, outputs, scratch, slot, remotes, locals_, vmem, flops):
+    names = list(inputs) + list(outputs) + list(scratch)
+
+    def kernel(*refs):
+        ns = types.SimpleNamespace(**dict(zip(names, refs)))
+        ns.copies = Copies(*refs[len(names) :])
+        body(ns)
+        ns.copies.finish()
+
+    moved = sum(v.size * v.dtype.itemsize for v in [*inputs.values(), *outputs.values()])
+    results = pl.pallas_call(
+        kernel,
+        name=name,
+        out_shape=list(outputs.values()),
+        in_specs=[pl.BlockSpec(memory_space=pl.ANY)] * len(inputs),
+        out_specs=[pl.BlockSpec(memory_space=pl.ANY)] * len(outputs),
+        scratch_shapes=[
+            *scratch.values(),
+            pltpu.SemaphoreType.DMA((remotes,)),
+            pltpu.SemaphoreType.DMA((remotes,)),
+            pltpu.SemaphoreType.DMA((locals_,)),
+        ],
+        compiler_params=pltpu.CompilerParams(
+            collective_id=slot, has_side_effects=True, vmem_limit_bytes=vmem << 20
+        ),
+        cost_estimate=pl.CostEstimate(flops=flops, bytes_accessed=moved, transcendentals=0),
+    )(*inputs.values())
+    return dict(zip(outputs, results))
+
+
+def next_qkv(ns, place, blocks):
+    gather = Gather(ns.copies, place, ns.normed_v)
+    for stream in range(2):
+        gather.start(stream, blocks[stream]())
+    ns.load_wq.wait()
+    for stream in range(2):
+
+        def project(side):
+            at = gather.pair(stream, side)
+
+            def sink(cols, value):
+                ns.qkv_v[at, cols] = value.astype(BF)
+
+            times(lambda: ns.normed_v[at, :], ns.wq_v, 384, sink)
+
+        gather.wait_chip(stream)
+        project(place.side)
+        gather.forward(stream)
+        gather.wait_rest(stream)
+        project(1 - place.side)
+        here = pl.ds(stream * 4 * TOK, 4 * TOK)
+        ns.copies.store(ns.normed_v.at[here, :], ns.normed.at[here, :])
+        ns.copies.store(ns.qkv_v.at[here, :], ns.qkv.at[here, :])
+
+
+def fwd_mid(ns, place, gain):
+    copies = ns.copies
+    attn = Scatter(copies, place, ns, "attn_")
+    down = Scatter(copies, place, ns, "down_")
+    gather = Gather(copies, place, ns.mlp_v)
+    ns.load_wo.wait()
+    ns.load_mixed.wait()
+    for stream in range(2):
+
+        def product(side, sink):
+            at = gather.pair(stream, side)
+            times(lambda: ns.mixed_v[at, :], ns.wo_v, 512, sink)
+
+        attn.push(stream, product)
+    ns.load_hidden.wait()
+    for stream in range(2):
+        value = attn.result(stream)
+        ns.attn_out_v[stream] = value
+        resid = ns.hidden_v[stream] + norm(value, gain(1))
+        ns.resid_v[stream] = resid
+        gather.start(stream, norm(resid, gain(2)).astype(BF))
+    ns.load_wu.wait()
+    ns.load_wd.wait()
+    for stream in range(2):
+
+        def expand(side):
+            at = gather.pair(stream, side)
+
+            def sink(cols, value):
+                active, slope = gelu_both(value)
+                ns.active_v[at, cols] = active.astype(BF)
+                ns.slope_v[at, cols] = slope.astype(BF)
+
+            times(lambda: ns.mlp_v[at, :], ns.wu_v, 256, sink)
+
+        gather.wait_chip(stream)
+        expand(place.side)
+        gather.forward(stream)
+        gather.wait_rest(stream)
+        expand(1 - place.side)
+
+        def product(side, sink):
+            at = gather.pair(stream, side)
+            times(lambda: ns.active_v[at, :], ns.wd_v, 512, sink)
+
+        down.push(stream, product)
+    return down
+
+
+def bwd_mid(ns, place, gain, grads):
+    copies = ns.copies
+    up = Scatter(copies, place, ns, "up_")
+    first = Gather(copies, place, ns.down_grad_v)
+    second = Gather(copies, place, ns.attn_grad_v)
+    for stream in range(2):
+        grad = grads[stream]()
+        ns.grad_v[stream] = grad
+        back, four = norm_back_in(ns.down_out_v[stream], gain(3), grad)
+        ns.dg_v[3:4, :] += four
+        first.start(stream, back.astype(BF))
+    for stream in range(2):
+
+        def shrink(side):
+            at = first.pair(stream, side)
+
+            def sink(cols, value):
+                slope = ns.slope_v[at, cols].astype(F32)
+                ns.up_grad_v[at, cols] = (value * slope).astype(BF)
+
+            times_rows(lambda: ns.down_grad_v[at, :], ns.wd_v, 512, sink)
+
+        first.wait_chip(stream)
+        shrink(place.side)
+        first.forward(stream)
+        first.wait_rest(stream)
+        shrink(1 - place.side)
+
+        def product(side, sink):
+            at = first.pair(stream, side)
+            times_rows(lambda: ns.up_grad_v[at, :], ns.wu_v, 512, sink)
+
+        up.push(stream, product)
+    gram(ns.active_v, ns.down_grad_v, 256, ns.gd_v)
+    copies.store(ns.gd_v, ns.gd)
+    for stream in range(2):
+        back, three = norm_back_in(ns.resid_v[stream], gain(2), up.result(stream))
+        grad = ns.grad_v[stream] + back
+        ns.grad_v[stream] = grad
+        ns.dg_v[2:3, :] += three
+        back, two = norm_back_in(ns.attn_out_v[stream], gain(1), grad)
+        ns.dg_v[1:2, :] += two
+        second.start(stream, back.astype(BF))
+    copies.store(ns.grad_v, ns.resid_grad)
+    gram(ns.mlp_v, ns.up_grad_v, 256, ns.gu_v)
+    copies.store(ns.gu_v, ns.gu)
+    for stream in range(2):
+
+        def project(side):
+            at = second.pair(stream, side)
+            ns.mixed_grad_v[at, :] = dot_nt(ns.attn_grad_v[at, :], ns.wo_v[...]).astype(BF)
+
+        second.wait_chip(stream)
+        project(place.side)
+        second.forward(stream)
+        second.wait_rest(stream)
+        project(1 - place.side)
+        here = pl.ds(stream * 4 * TOK, 4 * TOK)
+        copies.store(ns.mixed_grad_v.at[here, :], ns.mixed_grad.at[here, :])
+    ns.go_v[...] = dot_tn(ns.mixed_v[...], ns.attn_grad_v[...]).astype(BF)
+    copies.store(ns.go_v, ns.go)
+
+
+def bwd_head(ns, place, gain):
+    copies = ns.copies
+    qkv = Scatter(copies, place, ns, "qkv_")
+    walk = Gather(copies, place, None)
+    ns.load_wq.wait()
+    ns.load_qkv_grad.wait()
+    for stream in range(2):
+
+        def product(side, sink):
+            at = walk.pair(stream, side)
+            times_rows(lambda: ns.qkv_grad_v[at, :], ns.wq_v, 512, sink)
+
+        qkv.push(stream, product)
+    ns.load_normed.wait()
+    gram(ns.normed_v, ns.qkv_grad_v, 256, ns.gq_v)
+    copies.store(ns.gq_v, ns.gq)
+    ns.load_hidden.wait()
+    ns.load_grad_in.wait()
+
+    def result(stream):
+        back, one = norm_back_in(ns.hidden_v[stream], gain(0), qkv.result(stream))
+        ns.dg_head_v[...] += one
+        return ns.grad_in_v[stream] + back
+
+    return [functools.partial(result, stream) for stream in range(2)]
+
+
+def struct(shape, dtype):
+    return jax.ShapeDtypeStruct(shape, dtype)
+
+
+def load(ns, *names):
+    for name in names:
+        setattr(ns, "load_" + name, ns.copies.local(getattr(ns, name), getattr(ns, name + "_v")))
+
+
+def start_kernel(hidden, wq, gains):
+    width, part = wq.shape
+    length = 8 * TOK
+    inputs = dict(hidden=hidden, wq=wq, gains=gains)
+    outputs = dict(normed=struct((length, width), BF), qkv=struct((length, part), BF))
+    scratch = dict(
+        hidden_v=pltpu.VMEM((2, TOK, width), F32),
+        wq_v=pltpu.VMEM(wq.shape, BF),
+        gains_v=pltpu.VMEM(gains.shape, F32),
+        normed_v=pltpu.VMEM((length, width), BF),
+        qkv_v=pltpu.VMEM((length, part), BF),
+    )
+
+    def body(ns):
+        place = Place()
+        load(ns, "hidden", "gains", "wq")
+        meet([place.core, place.near])
+        ns.load_hidden.wait()
+        ns.load_gains.wait()
+        blocks = [
+            functools.partial(
+                lambda s: norm(ns.hidden_v[s], ns.gains_v[0:1, :]).astype(BF), stream
+            )
+            for stream in range(2)
+        ]
+        next_qkv(ns, place, blocks)
+
+    return launch("start", body, inputs, outputs, scratch, 0, 8, 8, 60, 2 * length * width * part)
+
+
+def forward_kernel(layer, mixed, hidden, gains, weights, wq):
+    wo, wu, wd = weights
+    width, units = wu.shape
+    part = wq.shape[1]
+    length = 8 * TOK
+    inputs = dict(mixed=mixed, hidden=hidden, gains=gains, wo=wo, wu=wu, wd=wd, wq=wq)
+    blocks = struct((2, TOK, width), F32)
+    wide = struct((length, width), BF)
+    outputs = dict(
+        attn_out=blocks,
+        resid=blocks,
+        mlp=wide,
+        active=struct((length, units), BF),
+        slope=struct((length, units), BF),
+        down_out=blocks,
+        hidden_out=blocks,
+        normed=wide,
+        qkv=struct((length, part), BF),
+    )
+    scratch = {
+        name + "_v": pltpu.VMEM(value.shape, value.dtype)
+        for name, value in {**inputs, **outputs}.items()
+    }
+    scratch |= scatter_scratch("attn_", width) | scatter_scratch("down_", width)
+
+    def body(ns):
+        place = Place()
+        load(ns, "mixed", "wo", "gains", "hidden", "wu", "wd", "wq")
+        meet([place.core, place.near])
+        ns.load_gains.wait()
+
+        def gain(index, level=layer):
+            return ns.gains_v[level * 4 + index : level * 4 + index + 1, :]
+
+        down = fwd_mid(ns, place, gain)
+        for name in ("attn_out", "resid", "mlp", "active", "slope"):
+            ns.copies.store(getattr(ns, name + "_v"), getattr(ns, name))
+
+        def block(stream):
+            value = down.result(stream)
+            ns.down_out_v[stream] = value
+            hidden_out = ns.resid_v[stream] + norm(value, gain(3))
+            ns.hidden_out_v[stream] = hidden_out
+            return norm(hidden_out, gain(0, layer + 1)).astype(BF)
+
+        next_qkv(ns, place, [functools.partial(block, stream) for stream in range(2)])
+        for name in ("down_out", "hidden_out"):
+            ns.copies.store(getattr(ns, name + "_v"), getattr(ns, name))
+
+    flops = 2 * length * width * (wo.shape[0] + 2 * units + part)
+    return launch("forward", body, inputs, outputs, scratch, 1, 32, 32, 60, flops)
+
+
+def turn_kernel(layer, mixed, hidden, gains, weights, cotangent):
+    wo, wu, wd = weights
+    width, units = wu.shape
+    length = 8 * TOK
+    inputs = dict(mixed=mixed, hidden=hidden, gains=gains, wo=wo, wu=wu, wd=wd, cot=cotangent)
+    blocks = struct((2, TOK, width), F32)
+    outputs = dict(
+        out=struct((2, TOK, width), BF),
+        resid_grad=blocks,
+        mixed_grad=struct(mixed.shape, BF),
+        gd=struct(wd.shape, BF),
+        gu=struct(wu.shape, BF),
+        go=struct(wo.shape, BF),
+        dg=struct((8, width), F32),
+    )
+    kept = dict(
+        attn_out=blocks,
+        resid=blocks,
+        grad=blocks,
+        mlp=struct((length, width), BF),
+        active=struct((length, units), BF),
+        slope=struct((length, units), BF),
+        up_grad=struct((length, units), BF),
+        down_out=blocks,
+        down_grad=struct((length, width), BF),
+        attn_grad=struct((length, width), BF),
+    )
+    scratch = {
+        name + "_v": pltpu.VMEM(value.shape, value.dtype)
+        for name, value in {**inputs, **outputs, **kept}.items()
+        if name != "resid_grad"
+    }
+    for name in ("attn_", "down_", "up_"):
+        scratch |= scatter_scratch(name, width)
+
+    def body(ns):
+        place = Place()
+        load(ns, "mixed", "wo", "gains", "hidden", "wu", "wd", "cot")
+        meet([place.core, place.near])
+        ns.load_gains.wait()
+        ns.dg_v[...] = jnp.zeros_like(ns.dg_v)
+
+        def gain(index):
+            return ns.gains_v[layer * 4 + index : layer * 4 + index + 1, :]
+
+        down = fwd_mid(ns, place, gain)
+        ns.load_cot.wait()
+
+        def grad(stream):
+            value = down.result(stream)
+            ns.down_out_v[stream] = value
+            return ns.cot_v[stream].astype(F32)
+
+        bwd_mid(ns, place, gain, [functools.partial(grad, stream) for stream in range(2)])
+        for stream in range(2):
+            out = ns.resid_v[stream] + norm(ns.down_out_v[stream], gain(3))
+            ns.out_v[stream] = out.astype(BF)
+        ns.copies.store(ns.out_v, ns.out)
+        ns.copies.store(ns.dg_v, ns.dg)
+
+    flops = 6 * length * width * (wo.shape[0] + 2 * units)
+    return launch("turn", body, inputs, outputs, scratch, 2, 48, 32, 62, flops)
+
+
+def backward_kernel(layer, qkv_grad, wq, normed, hidden, grad_in, gains, saved, weights):
+    wo, wu, wd = weights
+    width, units = wu.shape
+    length = 8 * TOK
+    inputs = dict(
+        qkv_grad=qkv_grad, wq=wq, normed=normed, hidden=hidden, grad_in=grad_in, gains=gains,
+        wo=wo, wu=wu, wd=wd, **saved,
+    )
+    blocks = struct((2, TOK, width), F32)
+    outputs = dict(
+        resid_grad=blocks,
+        mixed_grad=struct((length, wo.shape[0]), BF),
+        gq=struct(wq.shape, BF),
+        gd=struct(wd.shape, BF),
+        gu=struct(wu.shape, BF),
+        go=struct(wo.shape, BF),
+        dg=struct((8, width), F32),
+        dg_head=struct((1, width), F32),
+    )
+    kept = dict(
+        grad=blocks,
+        up_grad=struct((length, units), BF),
+        down_grad=struct((length, width), BF),
+        attn_grad=struct((length, width), BF),
+    )
+    scratch = {
+        name + "_v": pltpu.VMEM(value.shape, value.dtype)
+        for name, value in {**inputs, **outputs, **kept}.items()
+        if name != "resid_grad"
+    }
+    for name in ("qkv_", "up_"):
+        scratch |= scatter_scratch(name, width)
+
+    def body(ns):
+        place = Place()
+        load(ns, "qkv_grad", "wq", "gains", "normed", "hidden", "grad_in")
+        load(ns, "wd", "slope", "wu", "active", *(n for n in saved if n not in ("slope", "active")), "wo")
+        meet([place.core, place.near])
+        ns.load_gains.wait()
+        ns.dg_v[...] = jnp.zeros_like(ns.dg_v)
+        ns.dg_head_v[...] = jnp.zeros_like(ns.dg_head_v)
+
+        def gain(index, level=layer):
+            return ns.gains_v[level * 4 + index : level * 4 + index + 1, :]
+
+        grads = bwd_head(ns, place, lambda index: gain(index, layer + 1))
+        for name in ("wd", "wu", "wo", *saved):
+            getattr(ns, "load_" + name).wait()
+        bwd_mid(ns, place, gain, grads)
+        ns.copies.store(ns.dg_v, ns.dg)
+        ns.copies.store(ns.dg_head_v, ns.dg_head)
+
+    flops = 6 * length * width * (wo.shape[0] + 2 * units) + 4 * length * width * wq.shape[1]
+    return launch("backward", body, inputs, outputs, scratch, 3, 48, 48, 62, flops)
+
+
+def last_kernel(qkv_grad, wq, normed, hidden, grad_in, gains):
+    width = wq.shape[0]
+    inputs = dict(
+        qkv_grad=qkv_grad, wq=wq, normed=normed, hidden=hidden, grad_in=grad_in, gains=gains
+    )
+    outputs = dict(
+        out=struct((2, TOK, width), BF), gq=struct(wq.shape, BF), dg_head=struct((1, width), F32)
+    )
+    scratch = {
+        name + "_v": pltpu.VMEM(value.shape, value.dtype)
+        for name, value in {**inputs, **outputs}.items()
+    }
+    scratch |= scatter_scratch("qkv_", width)
+
+    def body(ns):
+        place = Place()
+        load(ns, "qkv_grad", "wq", "gains", "normed", "hidden", "grad_in")
+        meet([place.core, place.near])
+        ns.load_gains.wait()
+        ns.dg_head_v[...] = jnp.zeros_like(ns.dg_head_v)
+        grads = bwd_head(ns, place, lambda index: ns.gains_v[index : index + 1, :])
+        for stream in range(2):
+            ns.out_v[stream] = grads[stream]().astype(BF)
+        ns.copies.store(ns.out_v, ns.out)
+        ns.copies.store(ns.dg_head_v, ns.dg_head)
+
+    flops = 4 * 8 * TOK * width * wq.shape[1]
+    return launch("last", body, inputs, outputs, scratch, 4, 16, 16, 60, flops)
 
 
 def spread_rep(mine, rep):
@@ -243,19 +853,19 @@
     place, upper = grp % 4, grp // 4
 
     gains = lax.all_gather(norm_gains, "grp", axis=1, tiled=True).astype(F32)
-    gains = jnp.transpose(gains, (0, 2, 1))
+    gains = jnp.transpose(gains, (0, 2, 1)).reshape(layers * 4, width)
 
     def bring(two):
         mine = pick(two[:, 0], upper)
         other = far(pick(two[:, 0], 1 - upper))
-        return jnp.where(upper == 0, jnp.stack([mine, other]), jnp.stack([other, mine])).astype(F32)
+        return jnp.where(upper == 0, jnp.stack([mine, other]), jnp.stack([other, mine]))
 
     def send_back(mine):
         keep = pick(mine, upper)
         other = far(pick(mine, 1 - upper))
         return jnp.where(upper == 0, jnp.stack([keep, other]), jnp.stack([other, keep]))
 
-    hidden = bring(block_in).reshape(2 * tokens, width)
+    first = bring(block_in).astype(F32)
     weights = []
     for layer in range(layers):
         weights.append(
@@ -266,63 +876,44 @@
                 rows_in(w_down[layer], upper),
             )
         )
-
-    def gather(values):
-        return gather4(values.reshape(2, tokens, width), place)
-
-    saved = []
-    for layer in range(layers):
-        qkv_w, out_w, up_w, down_w = weights[layer]
-        gain = gains[layer]
-        normed = gather(norm(hidden, gain[0]).astype(BF))
-        qkv = dot(normed, qkv_w).astype(BF)
-        mixed, lse = attend(qkv)
-        attn_out = scatter4(dot(mixed, out_w), place)
-        resid = hidden + norm(attn_out, gain[1])
-        mlp_in = gather(norm(resid, gain[2]).astype(BF))
-        up_out = dot(mlp_in, up_w)
-        active = jax.nn.gelu(up_out).astype(BF)
-        down_out = scatter4(dot(active, down_w), place)
-        saved.append((hidden, normed, qkv, mixed, lse, attn_out, resid, mlp_in, up_out, active, down_out))
-        hidden = resid + norm(down_out, gain[3])
-    block_out = send_back(hidden.astype(BF).reshape(2, tokens, width))[:, None]
-
-    grad = bring(cotangent).reshape(2 * tokens, width)
-    results = [None] * layers
-    gain_grads = [None] * layers
-    for layer in reversed(range(layers)):
-        qkv_w, out_w, up_w, down_w = weights[layer]
-        gain = gains[layer]
-        hidden, normed, qkv, mixed, lse, attn_out, resid, mlp_in, up_out, active, down_out = saved[layer]
-        down_grad, four = norm_back(down_out, gain[3], grad)
-        down_low = gather(down_grad.astype(BF))
-        down_w_grad = dot_tn(active, down_low).astype(BF)
-        active_grad = dot_nt(down_low, down_w)
-        unused, puller = jax.vjp(jax.nn.gelu, up_out)
-        up_low = puller(active_grad)[0].astype(BF)
-        up_w_grad = dot_tn(mlp_in, up_low).astype(BF)
-        mlp_grad = scatter4(dot_nt(up_low, up_w), place)
-        part, three = norm_back(resid, gain[2], mlp_grad)
-        resid_grad = grad + part
-        attn_grad, two = norm_back(attn_out, gain[1], resid_grad)
-        attn_low = gather(attn_grad.astype(BF))
-        out_w_grad = dot_tn(mixed, attn_low).astype(BF)
-        mixed_grad = dot_nt(attn_low, out_w).astype(BF)
-        qkv_grad = attend_back(qkv, lse, mixed_grad)
-        qkv_w_grad = dot_tn(normed, qkv_grad).astype(BF)
-        normed_grad = scatter4(dot_nt(qkv_grad, qkv_w), place)
-        part, one = norm_back(hidden, gain[0], normed_grad)
-        grad = resid_grad + part
-        gain_grads[layer] = jnp.stack([one, two, three, four], axis=1)
-        results[layer] = (
-            columns_out(qkv_w_grad, 6, rows, rep, place, upper),
-            rows_out(out_w_grad, rep, upper),
-            columns_out(up_w_grad, 2, hidden_unit, rep, place, upper),
-            rows_out(down_w_grad, rep, upper),
+    begun = start_kernel(first, weights[0][0], gains)
+    mixed_0, lse_0 = attend(begun["qkv"])
+    lower = forward_kernel(0, mixed_0, first, gains, weights[0][1:], weights[1][0])
+    mixed_1, lse_1 = attend(lower["qkv"])
+    upper_out = turn_kernel(
+        1, mixed_1, lower["hidden_out"], gains, weights[1][1:], bring(cotangent)
+    )
+    block_out = send_back(upper_out["out"])[:, None]
+    qkv_grad_1 = attend_back(lower["qkv"], lse_1, upper_out["mixed_grad"])
+    saved = {
+        name: lower[name] for name in ("down_out", "slope", "active", "resid", "attn_out", "mlp")
+    }
+    lower_out = backward_kernel(
+        0, qkv_grad_1, weights[1][0], lower["normed"], lower["hidden_out"], upper_out["resid_grad"],
+        gains, dict(saved, mixed=mixed_0), weights[0][1:],
+    )
+    qkv_grad_0 = attend_back(begun["qkv"], lse_0, lower_out["mixed_grad"])
+    last = last_kernel(
+        qkv_grad_0, weights[0][0], begun["normed"], first, lower_out["resid_grad"], gains
+    )
+    block_in_grad = send_back(last["out"]).astype(F32)[:, None]
+
+    gain_grad = jnp.concatenate(
+        [last["dg_head"], lower_out["dg"][1:4], lower_out["dg_head"], upper_out["dg"][1:4]]
+    )
+    gain_all = lax.psum(gain_grad, ("rep", "grp"))
+    gain_mine = lax.dynamic_slice_in_dim(gain_all, grp * rows, rows, 1)
+    gain_mine = jnp.transpose(gain_mine.reshape(layers, 4, rows), (0, 2, 1))
+    results = []
+    for gq, out in ((last["gq"], lower_out), (lower_out["gq"], upper_out)):
+        results.append(
+            (
+                columns_out(gq, 6, rows, rep, place, upper),
+                rows_out(out["go"], rep, upper),
+                columns_out(out["gu"], 2, hidden_unit, rep, place, upper),
+                rows_out(out["gd"], rep, upper),
+            )
         )
-    block_in_grad = send_back(grad.astype(BF).reshape(2, tokens, width)).astype(F32)[:, None]
-    gain_all = lax.psum(jnp.stack(gain_grads), ("rep", "grp"))
-    gain_mine = lax.dynamic_slice_in_dim(gain_all, grp * rows, rows, 1)
     stacked = [jnp.stack([results[layer][k] for layer in range(layers)]) for k in range(4)]
     return (block_out, block_in_grad, *stacked, gain_mine)
 
@@ -635,7 +1226,8 @@
     rep_size, grp_size = mesh.shape["rep"], mesh.shape["grp"]
 
     def body(block_in, cotangent, w_qkv, w_out, w_up, w_down, norm_gains):
-        fits = (rep_size, grp_size, block_in.shape[0]) == (4, 8, 2)
+        sizes = (rep_size, grp_size, block_in.shape[0], w_qkv.shape[0], block_in.shape[2])
+        fits = sizes == (4, 8, 2, 2, TOK)
         chosen = body_pairs if fits else body_general
         return chosen(block_in, cotangent, w_qkv, w_out, w_up, w_down, norm_gains)
 

time: 1040 us -> 1020 us (0.981)
  Pallas kernels: 30.9 us -> 263 us
  waiting for transfers between devices: 596 us -> 454 us
  matrix products: 87.6 us -> 0 us
  blocking collectives: 104 us -> 145 us
  local copies, waits for them, and re-layouts: 98.8 us -> 68.6 us
  starting transfers between devices: 55.7 us -> 34.2 us
  other arithmetic: 42.7 us -> 32 us
    pallas_call x0 -> x5, Pallas kernels: none -> 233 us  [launch(): pl.pallas_call(kernel, name=name, out_shape=list(outputs.values()), in_sp...]
    ppermute x72 -> x24, waiting for transfers between devices: 338 us -> 115 us  [flip(): return lax.ppermute(value, axis, [(i, i ^ bit) for i in range(size)])]
    dot_general x24 -> x0, matrix products: 87.6 us -> none  [the longest x8 31.4 us: dot_tn(): lax.dot_general(left, right, (((0,), (0,)), ((), ())), preferred_element_...]
    all_gather x4, waiting for transfers between devices: 25.9 us -> 91.5 us  [columns_in(): whole = lax.all_gather(quarter, 'grp', axis=0, tiled=False)]
    all_gather x1, blocking collectives: 18.7 us -> 60.5 us  [body_pairs(): gains = lax.all_gather(norm_gains, 'grp', axis=1, tiled=True).astype(F32)]
    unnamed x14, waiting for transfers between devices: 220 us -> 243 us
    ppermute x72 -> x24, starting transfers between devices: 54.1 us -> 33.5 us  [flip(): return lax.ppermute(value, axis, [(i, i ^ bit) for i in range(size)])]
    dynamic_update_slice x24 -> x0, local copies, waits for them, and re-layouts: 13.8 us -> none  [gather4(): whole = lax.dynamic_update_slice(whole, value[:, None], (0, where, 0, 0))]
  transfers between devices with their start and end apart: 85 -> 37, of which waited for: 41 -> 16; matrix products, arithmetic and copies ran while one was open for 16% -> 8% of each run, Pallas kernels for 1% -> 8%
where the time goes in v2:
time: 1020 us; the launch traced here: 1010 us
  waiting for transfers between devices  454 us (45%)
  Pallas kernels  263 us (26%)
  blocking collectives  145 us (14%)
  local copies, waits for them, and re-layouts  68.6 us (7%)
  starting transfers between devices  34.2 us (3%)
  other arithmetic  32 us (3%)
  between operations  15.6 us (2%)
    unnamed x14, waiting for transfers between devices  243 us
    pallas_call x5, Pallas kernels, launch(): pl.pallas_call(kernel, name=name, out_shape=list(outputs.values()), in_sp...  233 us
    ppermute x24, waiting for transfers between devices, flip(): return lax.ppermute(value, axis, [(i, i ^ bit) for i in range(size)])  115 us
    all_gather x4, waiting for transfers between devices, columns_in(): whole = lax.all_gather(quarter, 'grp', axis=0, tiled=False)  91.5 us
    all_gather x1, blocking collectives, body_pairs(): gains = lax.all_gather(norm_gains, 'grp', axis=1, tiled=True).astype(F32)  60.5 us
    psum x1, blocking collectives, body_pairs(): gain_all = lax.psum(gain_grad, ('rep', 'grp'))  41.3 us
    ppermute x24, starting transfers between devices, flip(): return lax.ppermute(value, axis, [(i, i ^ bit) for i in range(size)])  33.5 us
    all_gather x2, blocking collectives, columns_out(): return lax.all_gather(both, 'rep', axis=0, tiled=True).astype(F32)  24.7 us
  transfers between devices with their start and end apart: 37, of which 16 were waited for; matrix products, arithmetic and copies ran while one was open for 8% of the time, Pallas kernels for 8%

profile of v2, /device:TPU:0, one launch (start us, length us, event | category | flops | bytes accessed | tf_op | source)
XLA Modules:
  0.0 1012.4 jit_solution(3001850510906677684)
XLA Ops:
  7.2 2.5 fusion.11
  9.7 1.6 constant_dynamic-slice_fusion.12
  14.0 25.3 %all-gather.13.cloned.1.call-done = bf16[8,32,3072]{2,1,0:T(8,128)(2,1)} async-done(((bf16[1,32,3072]{2,1,0:T(8,128)(2,1)}), bf16[8,32,3072]{2,1,0:T(8,128)(2,1)}) %all-gather.13.cloned.1.call-update) | async-done | bytes 1572880 | tf_op jit(solution)/shard_map/all_gather | solution.py:801
  39.3 3.2 reshape.285
  42.5 2.4 dynamic-slice_reduce_fusion.3
  46.2 19.9 %all-gather.21.cloned.1.call-done = bf16[8,32,3072]{2,1,0:T(8,128)(2,1)} async-done(((bf16[1,32,3072]{2,1,0:T(8,128)(2,1)}), bf16[8,32,3072]{2,1,0:T(8,128)(2,1)}) %all-gather.21.cloned.1.call-update) | async-done | bytes 1572880 | tf_op jit(solution)/shard_map/all_gather | solution.py:801
  66.1 3.2 reshape.293
  69.3 2.4 dynamic-slice_reduce_fusion.2
  73.2 23.8 %all-gather.17.cloned.1.call-done = bf16[8,32,4096]{2,1,0:T(8,128)(2,1)} async-done(((bf16[1,32,4096]{2,1,0:T(8,128)(2,1)}), bf16[8,32,4096]{2,1,0:T(8,128)(2,1)}) %all-gather.17.cloned.1.call-update) | async-done | bytes 2097168 | tf_op jit(solution)/shard_map/all_gather | solution.py:801
  97.0 3.3 reshape.290
  100.3 3.6 dynamic-slice_reduce_fusion.1
  105.1 22.5 %all-gather.25.cloned.1.call-done = bf16[8,32,4096]{2,1,0:T(8,128)(2,1)} async-done(((bf16[1,32,4096]{2,1,0:T(8,128)(2,1)}), bf16[8,32,4096]{2,1,0:T(8,128)(2,1)}) %all-gather.25.cloned.1.call-update) | async-done | bytes 2097168 | tf_op jit(solution)/shard_map/all_gather | solution.py:801
  127.6 3.3 reshape.296
  130.9 3.6 dynamic-slice_reduce_fusion
  135.8 1.9 slice_bitcast_fusion
  137.7 2.0 collective-permute-start.2
  141.5 1.9 collective-permute-start.3
  144.4 1.9 dynamic-slice_bitcast_fusion.9
  146.3 1.9 collective-permute-start.5
  148.2 60.5 %all_gather.57 = bf16[2,1024,4]{1,2,0:T(4,128)(2,1)S(1)} all-gather(bf16[2,128,4]{1,2,0:T(4,128)(2,1)S(1)} %copy-done.22), channel_id=1, replica_groups=mesh['rep'=4,'grp'=8] {'grp'}, dimensions={1}, use_global_device_ids=true | all-gather | bytes 18432 | tf_op jit(solution)/shard_map/all_gather | solution.py:855
  208.7 1.8 dynamic-slice_bitcast_fusion.11
  211.1 54.2 %collective-permute-done.5 = bf16[128,1024]{1,0:T(8,128)(2,1)} collective-permute-done((bf16[128,1024]{1,0:T(8,128)(2,1)}, bf16[128,1024]{1,0:T(8,128)(2,1)}, u32[]{:S(2)}, u32[]{:S(2)}) %collective-permute-start.5) | collective-permute-done | bytes 262176 | tf_op jit(solution)/shard_map/ppermute | solution.py:21
  265.3 6.7 collective-permute-start
  272.0 2.1 maximum_select_fusion.5.refs_6_
  274.1 2.2 maximum_select_fusion.3.refs_3_.refs_6_
  276.3 2.2 maximum_select_fusion.4.refs_3_
  278.5 6.2 collective-permute-done
  285.7 2.3 maximum_select_fusion.refs_5_.refs_8_
  288.0 3.9 maximum_select_fusion.1.refs_5_
  291.9 15.7 %start.1 = (bf16[1024,1024]{1,0:T(8,128)(2,1)}, bf16[1024,768]{1,0:T(8,128)(2,1)}) custom-call(f32[2,128,1024]{2,1,0:T(8,128)} %fusion.refs_0_.refs_1_.refs_3_, bf16[1024,768]{1,0:T(8,128)(2,1)} %bitcast.241, f32[8,1024]{1,0:T(8,128)} %reshape.317.refs_2_.refs_5_), custom_call_target="tpu_custom_call" | custom-call | flops 1610612736 | bytes 6324224 | tf_op jit(solution)/shard_map/start/pallas_call | solution.py:368
  309.0 4.7 shard_map.126
  315.3 58.3 %forward.1 = (f32[2,128,1024]{2,1,0:T(8,128)}, f32[2,128,1024]{2,1,0:T(8,128)}, bf16[1024,1024]{1,0:T(8,128)(2,1)}, bf16[1024,1024]{1,0:T(8,128)(2,1)}, bf16[102...) custom-call(bf16[1024,256]{1,0:T(8,128)(2,1)} %copy-done.7, ...), custom_call_target="tpu_custom_call" | custom-call | flops 6442450944 | bytes 22052864 | tf_op jit(solution)/shard_map/forward/pallas_call | solution.py:368
  375.1 4.7 shard_map.127
  381.4 82.4 %turn.1 = (bf16[2,128,1024]{2,1,0:T(8,128)(2,1)}, f32[2,128,1024]{2,1,0:T(8,128)}, bf16[1024,256]{1,0:T(8,128)(2,1)}, bf16[1024,1024]{1,0:T(8,128)(2,1)}, bf16[1...) custom-call(bf16[1024,256]{1,0:T(8,128)(2,1)} %copy-done.10, ...), custom_call_target="tpu_custom_call" | custom-call | flops 14495514624 | bytes 13697024 | tf_op jit(solution)/shard_map/turn/pallas_call | solution.py:368
  465.9 10.5 %shard_map.128.refs_0_ = bf16[1024,768]{1,0:T(8,128)(2,1)S(1)} custom-call(bf16[1024,768]{1,0:T(8,128)(2,1)S(1)} %copy-done.4, f32[1024,128]{1,0:T(8,128)S(1)} %copy-done.9, bf16[1024,256]{1,0:T(8,128)(2,1)S(1)} %copy-done.13), custom_call_target="tpu_custom_call" | custom-call | flops 5368709120 | bytes 4194304 | tf_op jit(solution)/shard_map/pallas_call | solution.py:148
  477.6 57.2 %backward.1 = (f32[2,128,1024]{2,1,0:T(8,128)}, bf16[1024,256]{1,0:T(8,128)(2,1)}, bf16[1024,768]{1,0:T(8,128)(2,1)}, bf16[1024,1024]{1,0:T(8,128)(2,1)}, bf16[1...) custom-call(bf16[1024,768]{1,0:T(8,128)(2,1)} %copy-done.11, ...), custom_call_target="tpu_custom_call" | custom-call | flops 17716740096 | bytes 29954048 | tf_op jit(solution)/shard_map/backward/pallas_call | solution.py:368
  536.9 10.5 %shard_map.129.refs_0_ = bf16[1024,768]{1,0:T(8,128)(2,1)S(1)} custom-call(bf16[1024,768]{1,0:T(8,128)(2,1)S(1)} %copy-done.1, f32[1024,128]{1,0:T(8,128)S(1)} %copy-done.6, bf16[1024,256]{1,0:T(8,128)(2,1)S(1)} %copy-done.12), custom_call_target="tpu_custom_call" | custom-call | flops 5368709120 | bytes 4194304 | tf_op jit(solution)/shard_map/pallas_call | solution.py:148
  548.6 19.0 %last.1 = (bf16[2,128,1024]{2,1,0:T(8,128)(2,1)}, bf16[1024,768]{1,0:T(8,128)(2,1)}, f32[1,1024]{1,0:T(1,128)}) custom-call(bf16[1024,768]{1,0:T(8,128)(2,1)} %copy-done.2, bf16[1024,768]{1,0:T(8,128)(2,1)} %bitcast.242, bf16[1024,1024]{1,0:T(8,128)(2,1)} %get-tuple-element.58.refs_2_, f32[2,128,1024]{2,1,0:T(8,128)} %fusion.refs_0_.refs_1_.refs_3_, ...), custom_call_target="tpu_custom_call" | custom-call | flops 3221225472 | bytes 9474048 | tf_op jit(solution)/shard_map/last/pallas_call | solution.py:368
  569.5 243.1 %all-reduce.11.cloned.1.call-done = (bf16[8,4,32,768]{3,2,1,0:T(8,128)(2,1)}, bf16[8,4,32,768]{3,2,1,0:T(8,128)(2,1)}, bf16[2,4,32,1024]{3,2,1,0:T(8,128)(2,1)},...) async-done(((bf16[8,4,32,768]{3,2,1,0:T(8,128)(2,1)}, ...) | async-done | bytes 12582928
  813.5 2.5 collective-permute-start.23
  816.0 12.2 %collective-permute-done.23 = bf16[128,1024]{1,0:T(8,128)(2,1)S(1)} collective-permute-done((bf16[128,1024]{1,0:T(8,128)(2,1)S(1)}, bf16[128,1024]{1,0:T(8,128)(2,1)S(1)}, u32[]{:S(2)}, u32[]{:S(2)}) %collective-permute-start.23) | collective-permute-done | bytes 262176 | tf_op jit(solution)/shard_map/ppermute | solution.py:21
  828.2 1.7 fusion.2
  830.2 3.0 collective-permute-start.7
  833.2 41.3 %psum.7 = f32[8,1024]{1,0:T(8,128)S(1)} all-reduce(f32[8,1024]{1,0:T(8,128)S(1)} %pad_maximum_fusion), channel_id=1, replica_groups=mesh['rep'=4,'grp'=8] {'rep','grp'}, use_global_device_ids=true, to_apply=%region_8.9 | all-reduce | flops 8192 | bytes 65536 | tf_op jit(solution)/shard_map/psum | solution.py:904
  878.9 1.8 constant_dynamic-slice_fusion.15
  880.8 2.2 collective-permute-start.11
  883.9 1.9 constant_dynamic-slice_fusion.13
  885.8 14.4 %collective-permute-done.22 = bf16[128,1024]{1,0:T(8,128)(2,1)S(1)} collective-permute-done((bf16[128,1024]{1,0:T(8,128)(2,1)S(1)}, bf16[128,1024]{1,0:T(8,128)(2,1)S(1)}, u32[]{:S(2)}, u32[]{:S(2)}) %collective-permute-start.22) | collective-permute-done | bytes 262176 | tf_op jit(solution)/shard_map/ppermute | solution.py:21
  900.2 1.7 fusion.3
  902.9 2.9 collective-permute-start.15
  906.7 15.9 %collective-permute-done.19 = bf16[4,32,1024]{2,1,0:T(8,128)(2,1)S(1)} collective-permute-done((bf16[4,32,1024]{2,1,0:T(8,128)(2,1)S(1)}, bf16[4,32,1024]{2,1,0:T(8,128)(2,1)S(1)}, u32[]{:S(2)}, u32[]{:S(2)}) %collective-permute-start.19) | collective-permute-done | bytes 262176 | tf_op jit(solution)/shard_map/ppermute | solution.py:21
  926.2 5.2 collective-permute-done.20
  932.4 9.8 all_gather.67
  943.6 8.4 all_gather.66
  953.1 2.5 collective-permute-start.17
  955.9 2.8 collective-permute-done.17
  958.9 2.1 collective-permute-start.9
  962.7 1.8 collective-permute-done.9
  966.4 11.8 %all_gather.65 = bf16[128,3072]{1,0:T(8,128)(2,1)S(1)} all-gather(bf16[32,3072]{1,0:T(8,128)(2,1)S(1)} %reshape.304), channel_id=1, replica_groups=mesh['rep'=4,'grp'=8] {'rep'}, dimensions={0}, use_global_device_ids=true | all-gather | bytes 983040 | tf_op jit(solution)/shard_map/all_gather | solution.py:827
  978.2 12.9 %all_gather.64 = bf16[128,3072]{1,0:T(8,128)(2,1)S(1)} all-gather(bf16[32,3072]{1,0:T(8,128)(2,1)S(1)} %reshape.301), channel_id=1, replica_groups=mesh['rep'=4,'grp'=8] {'rep'}, dimensions={0}, use_global_device_ids=true | all-gather | bytes 983040 | tf_op jit(solution)/shard_map/all_gather | solution.py:827
  991.1 1.9 maximum_convert_fusion.2
  993.0 4.0 maximum_convert_fusion.1
  997.0 4.8 all-gather.29.cloned.1.call-done
  1001.8 3.8 maximum_convert_fusion
  (175 shorter events, 45.3 us)
Async XLA Ops:
  7.2 32.1 %all-gather.13.cloned.1.call-start = ((), (), s32[]{:S(2)}) async-start(), calls=%async_computation | async-start | bytes 1769472 | tf_op jit(solution)/shard_map/all_gather | solution.py:801
  7.2 5.0 copy-start.14
  11.4 54.7 %all-gather.21.cloned.1.call-start = ((), (), s32[]{:S(2)}) async-start(), calls=%async_computation.4 | async-start | bytes 1769472 | tf_op jit(solution)/shard_map/all_gather | solution.py:801
  12.1 84.8 %all-gather.17.cloned.1.call-start = ((), (), s32[]{:S(2)}) async-start(), calls=%async_computation.2 | async-start | bytes 2359296 | tf_op jit(solution)/shard_map/all_gather | solution.py:801
  13.1 114.5 %all-gather.25.cloned.1.call-start = ((), (), s32[]{:S(2)}) async-start(), calls=%async_computation.6 | async-start | bytes 2359296 | tf_op jit(solution)/shard_map/all_gather | solution.py:801
  13.9 277.9 %all-gather.15.cloned.1.call-start = ((), (), s32[]{:S(2)}) async-start(), calls=%async_computation.1 | async-start | bytes 1966080 | tf_op jit(solution)/shard_map/all_gather | solution.py:805
  46.1 269.2 %all-gather.23.cloned.1.call-start = ((), (), s32[]{:S(2)}) async-start(), calls=%async_computation.5 | async-start | bytes 1966080 | tf_op jit(solution)/shard_map/all_gather | solution.py:805
  73.0 242.4 %all-gather.19.cloned.1.call-start = ((), (), s32[]{:S(2)}) async-start(), calls=%async_computation.3 | async-start | bytes 2621440 | tf_op jit(solution)/shard_map/all_gather | solution.py:805
  105.1 276.4 %all-gather.27.cloned.1.call-start = ((), (), s32[]{:S(2)}) async-start(), calls=%async_computation.7 | async-start | bytes 2621440 | tf_op jit(solution)/shard_map/all_gather | solution.py:805
  135.7 676.9 %all-reduce.11.cloned.1.call-start = ((), (), s32[]{:S(2)}) async-start(), calls=%async_computation.12 | async-start | bytes 25165824
  135.8 3.9 copy-start.17
  137.7 10.5 %copy-start.22 = (bf16[2,128,4]{1,2,0:T(4,128)(2,1)S(1)}, bf16[2,128,4]{1,2,0:T(4,128)(2,1)}, u32[]{:S(2)}) copy-start(bf16[2,128,4]{1,2,0:T(4,128)(2,1)} %param.13) | copy-start | bytes 6148
  137.7 148.0 %collective-permute-start.2 = (bf16[512,1024]{1,0:T(8,128)(2,1)S(1)}, bf16[512,1024]{1,0:T(8,128)(2,1)S(1)}, u32[]{:S(2)}, u32[]{:S(2)}) collective-permute-start(bf16[512,1024]{1,0:T(8,128)(2,1)S(1)} %get-tuple-element.82), channel_id=1, source_target_pairs={{0,4},{1,5},{2,6},{3,7},{4,0},{5,1},{6,2},{7,3},{8,12},{9,13},{10,... | collective-permute-start | bytes 3145736 | tf_op jit(solution)/shard_map/ppermute | solution.py:21
  140.5 133.6 %collective-permute-start.1 = (bf16[128,1024]{1,0:T(8,128)(2,1)}, bf16[128,1024]{1,0:T(8,128)(2,1)}, u32[]{:S(2)}, u32[]{:S(2)}) collective-permute-start(bf16[128,1024]{1,0:T(8,128)(2,1)} %get-tuple-element.94), channel_id=1, source_target_pairs={{0,4},{1,5},{2,6},{3,7},{4,0},{5,1},{6,2},{7,3},{8,12},{9,13},{10,... | collective-permute-start | bytes 786440 | tf_op jit(solution)/shard_map/ppermute | solution.py:21
  141.5 134.8 %collective-permute-start.3 = (bf16[128,1024]{1,0:T(8,128)(2,1)}, bf16[128,1024]{1,0:T(8,128)(2,1)}, u32[]{:S(2)}, u32[]{:S(2)}) collective-permute-start(bf16[128,1024]{1,0:T(8,128)(2,1)} %get-tuple-element.93), channel_id=1, source_target_pairs={{0,4},{1,5},{2,6},{3,7},{4,0},{5,1},{6,2},{7,3},{8,12},{9,13},{10,... | collective-permute-start | bytes 786440 | tf_op jit(solution)/shard_map/ppermute | solution.py:21
  143.4 144.6 %collective-permute-start.4 = (bf16[512,1024]{1,0:T(8,128)(2,1)S(1)}, bf16[512,1024]{1,0:T(8,128)(2,1)}, u32[]{:S(2)}, u32[]{:S(2)}) collective-permute-start(bf16[512,1024]{1,0:T(8,128)(2,1)S(1)} %get-tuple-element.81), channel_id=1, source_target_pairs={{0,4},{1,5},{2,6},{3,7},{4,0},{5,1},{6,2},{7,3},{8,12},{9,13},{10,... | collective-permute-start | bytes 3145736 | tf_op jit(solution)/shard_map/ppermute | solution.py:21
  146.3 119.0 %collective-permute-start.5 = (bf16[128,1024]{1,0:T(8,128)(2,1)}, bf16[128,1024]{1,0:T(8,128)(2,1)}, u32[]{:S(2)}, u32[]{:S(2)}) collective-permute-start(bf16[128,1024]{1,0:T(8,128)(2,1)} %get-tuple-element.92), channel_id=1, source_target_pairs={{0,4},{1,5},{2,6},{3,7},{4,0},{5,1},{6,2},{7,3},{8,12},{9,13},{10,... | collective-permute-start | bytes 786440 | tf_op jit(solution)/shard_map/ppermute | solution.py:21
  265.3 19.4 %collective-permute-start = (bf16[128,1024]{1,0:T(8,128)(2,1)}, bf16[128,1024]{1,0:T(8,128)(2,1)S(1)}, u32[]{:S(2)}, u32[]{:S(2)}) collective-permute-start(bf16[128,1024]{1,0:T(8,128)(2,1)} %get-tuple-element.96), channel_id=1, source_target_pairs={{0,4},{1,5},{2,6},{3,7},{4,0},{5,1},{6,2},{7,3},{8,12},{9,13},{10,... | collective-permute-start | bytes 786440 | tf_op jit(solution)/shard_map/ppermute | solution.py:21
  307.6 1.4 copy-start
  313.7 0.8 copy-start.5
  314.5 0.8 copy-start.7
  373.7 1.4 copy-start.3
  379.8 0.8 copy-start.8
  380.6 0.8 copy-start.10
  381.4 82.4 %copy-start.4 = (bf16[1024,768]{1,0:T(8,128)(2,1)S(1)}, bf16[1024,768]{1,0:T(8,128)(2,1)}, u32[]{:S(2)}) copy-start(bf16[1024,768]{1,0:T(8,128)(2,1)} %get-tuple-element.42.qkv_ref) | copy-start | bytes 4718596
  463.9 1.0 copy-start.9
  464.9 1.0 copy-start.13
  476.5 1.1 copy-start.11
  477.6 57.2 %copy-start.1 = (bf16[1024,768]{1,0:T(8,128)(2,1)S(1)}, bf16[1024,768]{1,0:T(8,128)(2,1)}, u32[]{:S(2)}) copy-start(bf16[1024,768]{1,0:T(8,128)(2,1)} %get-tuple-element.40.qkv_ref) | copy-start | bytes 4718596
  534.8 1.0 copy-start.6
  535.9 1.0 copy-start.12
  547.4 1.1 copy-start.2
  567.6 0.7 copy-start.23
  567.6 262.4 %copy-start.15 = (bf16[2,128,1024]{2,1,0:T(8,128)(2,1)S(1)}, bf16[2,128,1024]{2,1,0:T(8,128)(2,1)}, u32[]{:S(2)}) copy-start(bf16[2,128,1024]{2,1,0:T(8,128)(2,1)} %get-tuple-element.45) | copy-start | bytes 1572868
  567.6 262.5 %copy-start.16 = (bf16[2,128,1024]{2,1,0:T(8,128)(2,1)S(1)}, bf16[2,128,1024]{2,1,0:T(8,128)(2,1)}, u32[]{:S(2)}) copy-start(bf16[2,128,1024]{2,1,0:T(8,128)(2,1)} %get-tuple-element.60) | copy-start | bytes 1572868
  567.6 265.5 %copy-start.18 = (f32[8,1024]{1,0:T(8,128)S(1)}, f32[8,1024]{1,0:T(8,128)}, u32[]{:S(2)}) copy-start(f32[8,1024]{1,0:T(8,128)} %get-tuple-element.72) | copy-start | bytes 98308
  567.6 265.5 %copy-start.19 = (f32[8,1024]{1,0:T(8,128)S(1)}, f32[8,1024]{1,0:T(8,128)}, u32[]{:S(2)}) copy-start(f32[8,1024]{1,0:T(8,128)} %get-tuple-element.70) | copy-start | bytes 98308
  567.6 265.5 %copy-start.20 = (f32[1,1024]{1,0:T(1,128)S(1)}, f32[1,1024]{1,0:T(1,128)}, u32[]{:S(2)}) copy-start(f32[1,1024]{1,0:T(1,128)} %get-tuple-element.71) | copy-start | bytes 12292
  567.6 265.5 %copy-start.21 = (f32[1,1024]{1,0:T(1,128)S(1)}, f32[1,1024]{1,0:T(1,128)}, u32[]{:S(2)}) copy-start(f32[1,1024]{1,0:T(1,128)} %get-tuple-element.69) | copy-start | bytes 12292
  567.7 425.3 %all-gather.35.cloned.1.call-start = ((), (), s32[]{:S(2)}) async-start(), calls=%async_computation.11 | async-start | bytes 1310720 | tf_op jit(solution)/shard_map/all_gather | solution.py:844
  813.5 14.7 %collective-permute-start.23 = (bf16[128,1024]{1,0:T(8,128)(2,1)S(1)}, bf16[128,1024]{1,0:T(8,128)(2,1)S(1)}, u32[]{:S(2)}, u32[]{:S(2)}) collective-permute-start(bf16[128,1024]{1,0:T(8,128)(2,1)S(1)} %dynamic-slice_bitcast_fusion), channel_id=1, source_target_pairs={{0,4},{1,5},{2,6},{3,7},{4,0},{5,1},{6,2},{7,3},{8,12},{9,13},{10,... | collective-permute-start | bytes 786440 | tf_op jit(solution)/shard_map/ppermute | solution.py:21
  829.9 163.0 %all-gather.33.cloned.1.call-start = ((), (), s32[]{:S(2)}) async-start(), calls=%async_computation.10 | async-start | bytes 1310720 | tf_op jit(solution)/shard_map/all_gather | solution.py:844
  830.0 45.1 %collective-permute-start.6 = (bf16[128,1024]{1,0:T(8,128)(2,1)S(1)}, bf16[128,1024]{1,0:T(8,128)(2,1)S(1)}, u32[]{:S(2)}, u32[]{:S(2)}) collective-permute-start(bf16[128,1024]{1,0:T(8,128)(2,1)S(1)} %get-tuple-element.90), channel_id=1, source_target_pairs={{0,4},{1,5},{2,6},{3,7},{4,0},{5,1},{6,2},{7,3},{8,12},{9,13},{10,... | collective-permute-start | bytes 786440 | tf_op jit(solution)/shard_map/ppermute | solution.py:21
  830.2 45.9 %collective-permute-start.7 = (bf16[128,1024]{1,0:T(8,128)(2,1)S(1)}, bf16[128,1024]{1,0:T(8,128)(2,1)S(1)}, u32[]{:S(2)}, u32[]{:S(2)}) collective-permute-start(bf16[128,1024]{1,0:T(8,128)(2,1)S(1)} %get-tuple-element.88), channel_id=1, source_target_pairs={{0,4},{1,5},{2,6},{3,7},{4,0},{5,1},{6,2},{7,3},{8,12},{9,13},{10,... | collective-permute-start | bytes 786440 | tf_op jit(solution)/shard_map/ppermute | solution.py:21
  878.1 22.1 %collective-permute-start.22 = (bf16[128,1024]{1,0:T(8,128)(2,1)S(1)}, bf16[128,1024]{1,0:T(8,128)(2,1)S(1)}, u32[]{:S(2)}, u32[]{:S(2)}) collective-permute-start(bf16[128,1024]{1,0:T(8,128)(2,1)S(1)} %dynamic-slice_bitcast_fusion.1), channel_id=1, source_target_pairs={{0,4},{1,5},{2,6},{3,7},{4,0},{5,1},{6,2},{7,3},{8,12},{9,13},{10,... | collective-permute-start | bytes 786440 | tf_op jit(solution)/shard_map/ppermute | solution.py:21
  880.8 74.9 %collective-permute-start.11 = (bf16[4,32,768]{2,1,0:T(8,128)(2,1)S(1)}, bf16[4,32,768]{2,1,0:T(8,128)(2,1)S(1)}, u32[]{:S(2)}, u32[]{:S(2)}) collective-permute-start(bf16[4,32,768]{2,1,0:T(8,128)(2,1)S(1)} %dynamic-slice_bitcast_fusion.12), channel_id=1, source_target_pairs={{0,4},{1,5},{2,6},{3,7},{4,0},{5,1},{6,2},{7,3},{8,12},{9,13},{10,... | collective-permute-start | bytes 589832 | tf_op jit(solution)/shard_map/ppermute | solution.py:21
  883.0 75.8 %collective-permute-start.8 = (bf16[4,32,768]{2,1,0:T(8,128)(2,1)S(1)}, bf16[4,32,768]{2,1,0:T(8,128)(2,1)S(1)}, u32[]{:S(2)}, u32[]{:S(2)}) collective-permute-start(bf16[4,32,768]{2,1,0:T(8,128)(2,1)S(1)} %dynamic-slice_bitcast_fusion.13), channel_id=1, source_target_pairs={{0,4},{1,5},{2,6},{3,7},{4,0},{5,1},{6,2},{7,3},{8,12},{9,13},{10,... | collective-permute-start | bytes 589832 | tf_op jit(solution)/shard_map/ppermute | solution.py:21
  901.9 95.1 %all-gather.31.cloned.1.call-start = ((), (), s32[]{:S(2)}) async-start(), calls=%async_computation.9 | async-start | bytes 1310720 | tf_op jit(solution)/shard_map/all_gather | solution.py:827
  902.0 20.6 %collective-permute-start.19 = (bf16[4,32,1024]{2,1,0:T(8,128)(2,1)S(1)}, bf16[4,32,1024]{2,1,0:T(8,128)(2,1)S(1)}, u32[]{:S(2)}, u32[]{:S(2)}) collective-permute-start(bf16[4,32,1024]{2,1,0:T(8,128)(2,1)S(1)} %dynamic-slice_bitcast_fusion.2), channel_id=1, source_target_pairs={{0,4},{1,5},{2,6},{3,7},{4,0},{5,1},{6,2},{7,3},{8,12},{9,13},{10,... | collective-permute-start | bytes 786440 | tf_op jit(solution)/shard_map/ppermute | solution.py:21
  902.9 21.1 %collective-permute-start.15 = (bf16[32,1024]{1,0:T(8,128)(2,1)S(1)}, bf16[32,1024]{1,0:T(8,128)(2,1)S(1)}, u32[]{:S(2)}, u32[]{:S(2)}) collective-permute-start(bf16[32,1024]{1,0:T(8,128)(2,1)S(1)} %dynamic-slice_bitcast_fusion.22), channel_id=1, source_target_pairs={{0,4},{1,5},{2,6},{3,7},{4,0},{5,1},{6,2},{7,3},{8,12},{9,13},{10,... | collective-permute-start | bytes 196616 | tf_op jit(solution)/shard_map/ppermute | solution.py:21
  906.7 24.9 %collective-permute-start.14 = (bf16[32,1024]{1,0:T(8,128)(2,1)S(1)}, bf16[32,1024]{1,0:T(8,128)(2,1)S(1)}, u32[]{:S(2)}, u32[]{:S(2)}) collective-permute-start(bf16[32,1024]{1,0:T(8,128)(2,1)S(1)} %dynamic-slice_bitcast_fusion.23), channel_id=1, source_target_pairs={{0,4},{1,5},{2,6},{3,7},{4,0},{5,1},{6,2},{7,3},{8,12},{9,13},{10,... | collective-permute-start | bytes 196616 | tf_op jit(solution)/shard_map/ppermute | solution.py:21
  922.6 30.4 %collective-permute-start.16 = (bf16[4,32,1024]{2,1,0:T(8,128)(2,1)S(1)}, bf16[4,32,1024]{2,1,0:T(8,128)(2,1)S(1)}, u32[]{:S(2)}, u32[]{:S(2)}) collective-permute-start(bf16[4,32,1024]{2,1,0:T(8,128)(2,1)S(1)} %dynamic-slice_bitcast_fusion.3), channel_id=1, source_target_pairs={{0,4},{1,5},{2,6},{3,7},{4,0},{5,1},{6,2},{7,3},{8,12},{9,13},{10,... | collective-permute-start | bytes 786440 | tf_op jit(solution)/shard_map/ppermute | solution.py:21
  924.0 7.4 collective-permute-start.20
  931.5 10.7 %collective-permute-start.21 = (bf16[2,32,1024]{2,1,0:T(8,128)(2,1)S(1)}, bf16[2,32,1024]{2,1,0:T(8,128)(2,1)S(1)}, u32[]{:S(2)}, u32[]{:S(2)}) collective-permute-start(bf16[2,32,1024]{2,1,0:T(8,128)(2,1)S(1)} %get-tuple-element.102), channel_id=1, source_target_pairs={{0,1},{1,0},{2,3},{3,2},{4,5},{5,4},{6,7},{7,6},{8,9},{9,8},{10,11... | collective-permute-start | bytes 393224 | tf_op jit(solution)/shard_map/ppermute | solution.py:21
  943.6 58.3 %all-gather.29.cloned.1.call-start = ((), (), s32[]{:S(2)}) async-start(), calls=%async_computation.8 | async-start | bytes 1310720 | tf_op jit(solution)/shard_map/all_gather | solution.py:827
  953.1 5.5 collective-permute-start.17
  955.8 6.5 collective-permute-start.12
  958.7 2.3 collective-permute-start.18
  958.9 5.5 collective-permute-start.9
  962.4 2.2 collective-permute-start.13
  964.5 1.4 collective-permute-start.10
Sparse Core Ops, SparseCore 0:
  11.5 27.7 all-gather.12
  41.5 24.5 all-gather.20
  68.3 28.6 all-gather.16
  99.0 28.5 all-gather.24
  129.9 30.4 all-gather.14
  162.1 30.9 all-gather.22
  195.5 35.2 all-gather.18
  232.7 35.2 all-gather.26
  567.7 244.7 all-reduce.10
  830.1 26.7 all-gather.34
  902.0 26.1 all-gather.32
  943.7 26.2 all-gather.30
  971.9 29.9 all-gather.28
